TPU v7x, 256 devices: a whole 4x4x8 slice. The times are simulated.
256 devices in a mesh: gx: 8 (over z_hi, core), gy: 4 (over x), gz: 8 (over y, z_lo).
Axes of the slice: x: 4, y: 4, z: 8 (z_hi: 4, z_lo: 2; z = z_hi * 2 + z_lo), core: 2. Of those that a mesh axis runs over, the one named last changes fastest.
Arguments:
- features: float32 [16, 8, 8, 128, 128], P('gx', 'gy', 'gz'), may hold values from -6 to 6
- positions: float32 [16, 8, 8, 3, 128], P('gx', 'gy', 'gz'), may hold values from 0 to 1
- counts: int32 [16, 8, 8], P('gx', 'gy', 'gz'), may hold values from 64 to 128, as said below
- waves: int32 [3, 2048], replicated, may hold values from -8 to 8
- filter_table: float32 [2048, 128], replicated, may hold values from -6 to 6
- w_value: float32 [128, 128], replicated, may hold values from -0.5 to 0.5
- w_charge: float32 [128, 128], replicated, may hold values from -0.5 to 0.5
- radial_mix: float32 [8, 128], replicated, may hold values from -2 to 2
- w_hidden: float32 [128, 256], replicated, may hold values from -0.5 to 0.5
- w_out: float32 [256, 128], replicated, may hold values from -0.375 to 0.375
Outputs:
- updated: float32 [16, 8, 8, 128, 128], P('gx', 'gy', 'gz')
Inputs may be any that keep to these rules, and one draw needn't show every extreme that they name: `counts`: slots below a cell's count hold atoms, the others are padding.
All inputs are finite; a program needn't handle non-finite values.
Results may differ from a plain program's by a relative error of at most 0.0001.
Values sent between devices are 32-bit elements; how exact they have to be, the bound alone decides.
A program may use at most 64 MiB of HBM per device.

v0:
```python
import math

import jax
import jax.numpy as jnp
from jax import lax
from jax.sharding import PartitionSpec as P

K = 2048
B = 8
A = 128


highest = lax.Precision.HIGHEST
cut_radius = 1.0
message_scale = 0.125


def with_halo(block, sides, width):
    for axis, dim in sides:
        count = lax.axis_size(axis)
        forward = [(i, i + 1) for i in range(count - 1)]
        forward.append((count - 1, 0))
        backward = [(target, source) for source, target in forward]
        low = lax.ppermute(
            lax.slice_in_dim(block, block.shape[dim] - width, None, axis=dim), axis, forward
        )
        high = lax.ppermute(lax.slice_in_dim(block, 0, width, axis=dim), axis, backward)
        block = jnp.concatenate([low, block, high], axis=dim)
    return block


def radial_kernel(own_pos, nearby_pos, shift, self_pair):
    offsets = shift[:, None, None] + nearby_pos[..., :, None, :] - own_pos[..., :, :, None]
    squared = jnp.sum(offsets * offsets, axis=-3)
    distance = jnp.sqrt(squared)
    envelope = jnp.square(jnp.maximum(1.0 - squared / (cut_radius * cut_radius), 0.0))
    envelope = envelope * (1.0 - self_pair * jnp.eye(A, dtype=jnp.float32))
    centres = jnp.arange(B, dtype=jnp.float32) * (cut_radius / (B - 1))
    scaled = (distance[..., None, :, :] - centres[:, None, None]) * ((B - 1) / cut_radius)
    return jnp.exp(-scaled * scaled) * envelope[..., None, :, :]


def pair_term(own_pos, nearby, shift, self_pair, radial_mix):
    channels = nearby.shape[-2] - 3
    kernel = radial_kernel(own_pos, nearby[..., channels:, :], shift, self_pair)
    weighted = radial_mix[:, :, None] * nearby[..., None, :channels, :]
    return jnp.einsum("...bij,...bcj->...ci", kernel, weighted, precision=highest)


def plane_waves(frac_x, frac_y, frac_z, waves):
    expand = (waves.shape[1],) + (1,) * frac_x.ndim
    wave_float = waves.astype(jnp.float32)
    angle = (
        wave_float[0].reshape(expand) * frac_x
        + wave_float[1].reshape(expand) * frac_y
        + wave_float[2].reshape(expand) * frac_z
    )
    angle = angle * (2.0 * math.pi)
    return (jnp.cos(angle), jnp.sin(angle))


def shards(
    features, positions, counts, waves, filter_table, w_value, w_charge, radial_mix, w_hidden, w_out
):
    cells_x, cells_y, cells_z = counts.shape
    slot_ids = lax.broadcasted_iota(jnp.int32, (cells_x, cells_y, cells_z, A), 3)
    present = (slot_ids < counts[..., None]).astype(jnp.float32)[..., None, :]
    values = jnp.einsum("dc,xyzda->xyzca", w_value, features, precision=highest) * present
    charges = jnp.einsum("dc,xyzda->xyzca", w_charge, features, precision=highest) * present
    packed = jnp.concatenate([values, positions], axis=3)
    padded = with_halo(packed, (("gx", 0), ("gy", 1), ("gz", 2)), 1)

    def add_offset(step, summed):
        shift_x = step // 9 - 1
        shift_y = step // 3 % 3 - 1
        shift_z = step % 3 - 1
        nearby = lax.dynamic_slice(
            padded, (shift_x + 1, shift_y + 1, shift_z + 1, 0, 0), packed.shape
        )
        shift = jnp.stack([shift_x, shift_y, shift_z]).astype(jnp.float32)
        self_pair = (step == 13).astype(jnp.float32)
        return summed + pair_term(positions, nearby, shift, self_pair, radial_mix)

    messages = lax.fori_loop(0, 27, add_offset, jnp.zeros_like(values))
    grid_x = cells_x * lax.axis_size("gx")
    grid_y = cells_y * lax.axis_size("gy")
    grid_z = cells_z * lax.axis_size("gz")
    cell_x = (lax.axis_index("gx") * cells_x).astype(jnp.float32) + lax.broadcasted_iota(
        jnp.float32, (cells_x, 1, 1, 1), 0
    )
    cell_y = (lax.axis_index("gy") * cells_y).astype(jnp.float32) + lax.broadcasted_iota(
        jnp.float32, (1, cells_y, 1, 1), 1
    )
    cell_z = (lax.axis_index("gz") * cells_z).astype(jnp.float32) + lax.broadcasted_iota(
        jnp.float32, (1, 1, cells_z, 1), 2
    )
    frac_x = (cell_x + positions[:, :, :, 0, :]) / grid_x
    frac_y = (cell_y + positions[:, :, :, 1, :]) / grid_y
    frac_z = (cell_z + positions[:, :, :, 2, :]) / grid_z
    cosine, sine = plane_waves(frac_x, frac_y, frac_z, waves)
    real_part = jnp.einsum("kxyza,xyzca->kc", cosine, charges, precision=highest)
    imag_part = jnp.einsum("kxyza,xyzca->kc", sine, charges, precision=highest)
    partial_factors = jnp.stack([real_part, imag_part])
    normalizer = 1.0 / math.sqrt(grid_x * grid_y * grid_z * A)
    factors = lax.psum(partial_factors, ("gx", "gy", "gz"))
    filtered = factors * normalizer * filter_table[None]
    first = jnp.einsum("kc,kxyza->xyzca", filtered[0], cosine, precision=highest)
    second = jnp.einsum("kc,kxyza->xyzca", filtered[1], sine, precision=highest)
    potentials = (first + second) * (1.0 / math.sqrt(K))
    mixed = features + message_scale * messages + potentials
    hidden = jax.nn.silu(jnp.einsum("cf,xyzca->xyzfa", w_hidden, mixed, precision=highest))
    return (mixed + jnp.einsum("fc,xyzfa->xyzca", w_out, hidden, precision=highest)) * present


def solution(mesh):
    placed = (
        P("gx", "gy", "gz", None, None),
        P("gx", "gy", "gz", None, None),
        P("gx", "gy", "gz"),
        P(),
        P(),
        P(),
        P(),
        P(),
        P(),
        P(),
    )
    return jax.shard_map(
        shards,
        mesh=mesh,
        in_specs=placed,
        out_specs=P("gx", "gy", "gz", None, None),
        check_vma=False,
    )
```

profile of v0, /device:TPU:1, one launch (start us, length us, event | category | flops | bytes accessed | tf_op | source)
XLA Modules:
  0.0 634.6 jit_solution(14829387296556383303)
XLA Ops:
  16.9 21.1 %fusion.38 = f32[1,2048,128]{2,1,0:T(8,128)S(1)} fusion(f32[2,2,128,128]{3,2,1,0:T(8,128)S(1)} %fusion.72, f32[2,2,128]{2,1,0:T(2,128)S(1)} %bitcast.145, f32[2048]{0:T(1024)S(1)} %bitcast.137, f32[2,2,128]{2,1,0:T(2,128)S(1)} %get-tuple-element.283, f32[2048]{0:T(1024)S(1)} %bitcast.141, f32[2,2,128]{2,1,0:T(2,128)S(1)} %get-tuple-element.284, ...), kind=kOutput, calls=%fused_computation.34 | convolution fusion | flops 1616904192 | bytes 1341440 | tf_op jit(solution)/shard_map/kxyza,xyzca->kc/dot_general | solution.py:101
  37.9 21.3 %fusion.35 = f32[1,2048,128]{2,1,0:T(8,128)S(1)} fusion(f32[2,2,128,128]{3,2,1,0:T(8,128)S(1)} %fusion.72, f32[2,2,128]{2,1,0:T(2,128)S(1)} %bitcast.146, f32[2048]{0:T(1024)S(1)} %bitcast.138, f32[2,2,128]{2,1,0:T(2,128)S(1)} %get-tuple-element.283, f32[2048]{0:T(1024)S(1)} %bitcast.142, f32[2,2,128]{2,1,0:T(2,128)S(1)} %get-tuple-element.284, ...), kind=kOutput, calls=%fused_computation.33 | convolution fusion | flops 1616904192 | bytes 1341440 | tf_op jit(solution)/shard_map/kxyza,xyzca->kc/dot_general | solution.py:102
  75.1 252.9 %all-reduce.2.cloned.1.call-done = f32[2,2048,128]{2,1,0:T(8,128)} async-done(((f32[2,2048,128]{2,1,0:T(8,128)}), f32[2,2048,128]{2,1,0:T(8,128)}) %all-reduce.2.cloned.1.call-update) | async-done | bytes 2097168 | tf_op jit(solution)/shard_map/psum | solution.py:105
  329.8 18.5 %fusion.27 = f32[2,2,128,128]{3,2,1,0:T(8,128)} fusion(f32[2,2,128]{2,1,0:T(2,128)S(1)} %bitcast.147, f32[2048]{0:T(1024)S(1)} %bitcast.139, f32[2,2,128]{2,1,0:T(2,128)S(1)} %get-tuple-element.283, f32[2048]{0:T(1024)S(1)} %bitcast.143, f32[2,2,128]{2,1,0:T(2,128)S(1)} %get-tuple-element.284, f32[2048]{0:T(1024)S(1)} %bitcast.135, ...), kind=kOutput, calls=%fused_computation.28 | convolution fusion | flops 1616904192 | bytes 1341440 | tf_op jit(solution)/shard_map/kc,kxyza->xyzca/dot_general | solution.py:107
  351.8 253.0 %while.19 = (s32[]{:T(128)}, f32[2,2,1,128,128]{4,3,1,0,2:T(8,128)}, f32[8,128]{1,0:T(8,128)S(1)}, f32[4,4,3,131,128]{4,3,1,0,2:T(8,128)S(1)}, f32[2,2,1,3,128]{...) while((s32[]{:T(128)}, ...), condition=%wide.region_2.3_spmd.clone, body=%wide.region_0.2_spmd.clone.sunk | while | flops 809420352 | bytes 28811984 | solution.py:84
  365.9 4.5 fusion.122
  375.2 4.5 fusion.122
  384.6 4.5 fusion.122
  394.0 4.5 fusion.122
  403.3 4.5 fusion.122
  412.7 4.5 fusion.122
  422.1 4.5 fusion.122
  431.4 4.5 fusion.122
  440.8 4.5 fusion.122
  450.2 4.5 fusion.122
  459.5 4.5 fusion.122
  468.9 4.5 fusion.122
  487.7 4.5 fusion.122
  506.4 4.5 fusion.122
  534.5 4.5 fusion.122
  553.2 4.5 fusion.122
  581.3 4.5 fusion.122
  600.1 4.5 fusion.122
  605.9 19.3 %fusion.82 = f32[2,2,1,128,128]{3,4,1,0,2:T(8,128)S(1)} fusion(f32[2,2,128,128]{3,2,1,0:T(8,128)} %fusion.27, f32[2,2,128]{2,1,0:T(2,128)S(1)} %bitcast.148, f32[2048]{0:T(1024)S(1)} %bitcast.140, f32[2,2,128]{2,1,0:T(2,128)S(1)} %get-tuple-element.283, f32[2048]{0:T(1024)S(1)} %bitcast.144, f32[2,2,128]{2,1,0:T(2,128)S(1)} %get-tuple-element.284, ...), kind=kOutput, calls=%fused_computation.75 | convolution fusion | flops 1617231872 | bytes 2127872 | tf_op jit(solution)/shard_map/kc,kxyza->xyzca/dot_general | solution.py:108
  (409 shorter events, 204.8 us)
Async XLA Ops:
  6.5 618.7 %copy-start = (f32[128,256]{1,0:T(8,128)S(1)}, f32[128,256]{1,0:T(8,128)}, u32[]{:S(2)}) copy-start(f32[128,256]{1,0:T(8,128)} %param.20) | copy-start | bytes 393220
  6.5 321.5 %all-reduce.2.cloned.1.call-start = ((), (), s32[]{:S(2)}) async-start(), calls=%async_computation | async-start | bytes 4194304 | tf_op jit(solution)/shard_map/psum | solution.py:105
  9.4 58.2 %copy-start.3 = (f32[2,2,1,128,128]{4,3,1,0,2:T(8,128)}, f32[2,2,1,128,128]{4,3,1,0,2:T(8,128)S(1)}, u32[]{:S(2)}) copy-start(f32[2,2,1,128,128]{4,3,1,0,2:T(8,128)S(1)} %fusion.70) | copy-start | bytes 786436
  9.4 51.3 %collective-permute-start = (f32[1,2,1,131,128]{4,3,1,0,2:T(8,128)S(1)}, f32[1,2,1,131,128]{4,3,1,0,2:T(8,128)S(1)}, u32[]{:S(2)}, u32[]{:S(2)}) collective-permute-start(f32[1,2,1,131,128]{4,3,1,0,2:T(8,128)S(1)} %get-tuple-element.275), channel_id=1, source_target_pairs={{0,32},{32,64},{64,96},{96,128},{128,160},{160,192},{192,224},{224... | collective-permute-start | bytes 402440 | tf_op jit(solution)/shard_map/ppermute | solution.py:24
  13.9 46.8 %collective-permute-start.1 = (f32[1,2,1,131,128]{4,3,1,0,2:T(8,128)S(1)}, f32[1,2,1,131,128]{4,3,1,0,2:T(8,128)S(1)}, u32[]{:S(2)}, u32[]{:S(2)}) collective-permute-start(f32[1,2,1,131,128]{4,3,1,0,2:T(8,128)S(1)} %get-tuple-element.276), channel_id=1, source_target_pairs={{32,0},{64,32},{96,64},{128,96},{160,128},{192,160},{224,192},{0,2... | collective-permute-start | bytes 402440 | tf_op jit(solution)/shard_map/ppermute | solution.py:27
  60.7 13.4 %copy-start.15 = (f32[2048,128]{1,0:T(8,128)S(1)}, f32[2048,128]{1,0:T(8,128)}, u32[]{:S(2)}) copy-start(f32[2048,128]{1,0:T(8,128)} %param.16) | copy-start | bytes 3145732
  60.7 10.4 %copy-start.7 = (f32[1,2,1,131,128]{4,3,1,0,2:T(8,128)}, f32[1,2,1,131,128]{4,3,1,0,2:T(8,128)S(1)}, u32[]{:S(2)}) copy-start(f32[1,2,1,131,128]{4,3,1,0,2:T(8,128)S(1)} %collective-permute-done) | copy-start | bytes 402436
  60.7 10.4 %copy-start.9 = (f32[1,2,1,131,128]{4,3,1,0,2:T(8,128)}, f32[1,2,1,131,128]{4,3,1,0,2:T(8,128)S(1)}, u32[]{:S(2)}) copy-start(f32[1,2,1,131,128]{4,3,1,0,2:T(8,128)S(1)} %collective-permute-done.1) | copy-start | bytes 402436
  60.8 13.4 %copy-start.16 = (f32[2,2,1,3,128]{4,2,3,1,0:T(1,128)S(1)}, f32[2,2,1,3,128]{4,2,3,1,0:T(1,128)}, u32[]{:S(2)}) copy-start(f32[2,2,1,3,128]{4,2,3,1,0:T(1,128)} %param.13) | copy-start | bytes 18436
  60.8 13.4 %copy-start.5 = (f32[2,2,1,128,128]{4,3,2,1,0:T(8,128)S(1)}, f32[2,2,1,128,128]{4,3,2,1,0:T(8,128)}, u32[]{:S(2)}) copy-start(f32[2,2,1,128,128]{4,3,2,1,0:T(8,128)} %param.12) | copy-start | bytes 786436
  60.8 6.7 %collective-permute-start.2 = (f32[4,1,1,131,128]{4,3,1,0,2:T(8,128)S(1)}, f32[4,1,1,131,128]{4,3,1,0,2:T(8,128)S(1)}, u32[]{:S(2)}, u32[]{:S(2)}) collective-permute-start(f32[4,1,1,131,128]{4,3,1,0,2:T(8,128)S(1)} %get-tuple-element.273), channel_id=1, source_target_pairs={{0,8},{8,16},{16,24},{24,0},{1,9},{9,17},{17,25},{25,1},{2,10},{10... | collective-permute-start | bytes 804872 | tf_op jit(solution)/shard_map/ppermute | solution.py:24
  62.1 5.4 collective-permute-start.3
  68.7 279.6 %collective-permute-start.4 = (f32[4,4,1,131,128]{4,1,3,2,0:T(4,128)S(1)}, f32[4,4,1,131,128]{4,1,3,2,0:T(4,128)}, u32[]{:S(2)}, u32[]{:S(2)}) collective-permute-start(f32[4,4,1,131,128]{4,1,3,2,0:T(4,128)S(1)} %copy.49), channel_id=1, source_target_pairs={{0,1},{1,2},{2,3},{3,4},{4,5},{5,6},{6,7},{7,0},{8,9},{9,10},{10,1... | collective-permute-start | bytes 3219464 | tf_op jit(solution)/shard_map/ppermute | solution.py:24
  71.1 278.5 %collective-permute-start.5 = (f32[4,4,1,131,128]{4,1,3,2,0:T(4,128)S(1)}, f32[4,4,1,131,128]{4,1,3,2,0:T(4,128)}, u32[]{:S(2)}, u32[]{:S(2)}) collective-permute-start(f32[4,4,1,131,128]{4,1,3,2,0:T(4,128)S(1)} %copy.49), channel_id=1, source_target_pairs={{1,0},{2,1},{3,2},{4,3},{5,4},{6,5},{7,6},{0,7},{9,8},{10,9},{11,1... | collective-permute-start | bytes 3219464 | tf_op jit(solution)/shard_map/ppermute | solution.py:27
  329.8 18.5 %copy-start.6 = (f32[2,2048,128]{2,1,0:T(8,128)}, f32[2,2048,128]{2,1,0:T(8,128)S(1)}, u32[]{:S(2)}) copy-start(f32[2,2048,128]{2,1,0:T(8,128)S(1)} %broadcast_multiply_fusion) | copy-start | bytes 6291460
  364.0 6.4 %copy-start.2 = (f32[4,4,3,131,128]{4,3,1,0,2:T(8,128)S(1)}, f32[4,4,3,131,128]{4,3,1,0,2:T(8,128)}, u32[]{:S(2)}) copy-start(f32[4,4,3,131,128]{4,3,1,0,2:T(8,128)} %copy-done.1) | copy-start | bytes 9658372 | tf_op jit(solution)/shard_map/while
  392.2 6.4 %copy-start.2 = (f32[4,4,3,131,128]{4,3,1,0,2:T(8,128)S(1)}, f32[4,4,3,131,128]{4,3,1,0,2:T(8,128)}, u32[]{:S(2)}) copy-start(f32[4,4,3,131,128]{4,3,1,0,2:T(8,128)} %copy-done.1) | copy-start | bytes 9658372 | tf_op jit(solution)/shard_map/while
  410.9 6.4 %copy-start.2 = (f32[4,4,3,131,128]{4,3,1,0,2:T(8,128)S(1)}, f32[4,4,3,131,128]{4,3,1,0,2:T(8,128)}, u32[]{:S(2)}) copy-start(f32[4,4,3,131,128]{4,3,1,0,2:T(8,128)} %copy-done.1) | copy-start | bytes 9658372 | tf_op jit(solution)/shard_map/while
  439.0 6.4 %copy-start.2 = (f32[4,4,3,131,128]{4,3,1,0,2:T(8,128)S(1)}, f32[4,4,3,131,128]{4,3,1,0,2:T(8,128)}, u32[]{:S(2)}) copy-start(f32[4,4,3,131,128]{4,3,1,0,2:T(8,128)} %copy-done.1) | copy-start | bytes 9658372 | tf_op jit(solution)/shard_map/while
  485.8 6.4 %copy-start.2 = (f32[4,4,3,131,128]{4,3,1,0,2:T(8,128)S(1)}, f32[4,4,3,131,128]{4,3,1,0,2:T(8,128)}, u32[]{:S(2)}) copy-start(f32[4,4,3,131,128]{4,3,1,0,2:T(8,128)} %copy-done.1) | copy-start | bytes 9658372 | tf_op jit(solution)/shard_map/while
  532.7 6.4 %copy-start.2 = (f32[4,4,3,131,128]{4,3,1,0,2:T(8,128)S(1)}, f32[4,4,3,131,128]{4,3,1,0,2:T(8,128)}, u32[]{:S(2)}) copy-start(f32[4,4,3,131,128]{4,3,1,0,2:T(8,128)} %copy-done.1) | copy-start | bytes 9658372 | tf_op jit(solution)/shard_map/while
  551.4 6.4 %copy-start.2 = (f32[4,4,3,131,128]{4,3,1,0,2:T(8,128)S(1)}, f32[4,4,3,131,128]{4,3,1,0,2:T(8,128)}, u32[]{:S(2)}) copy-start(f32[4,4,3,131,128]{4,3,1,0,2:T(8,128)} %copy-done.1) | copy-start | bytes 9658372 | tf_op jit(solution)/shard_map/while
  598.2 6.4 %copy-start.2 = (f32[4,4,3,131,128]{4,3,1,0,2:T(8,128)S(1)}, f32[4,4,3,131,128]{4,3,1,0,2:T(8,128)}, u32[]{:S(2)}) copy-start(f32[4,4,3,131,128]{4,3,1,0,2:T(8,128)} %copy-done.1) | copy-start | bytes 9658372 | tf_op jit(solution)/shard_map/while
  605.9 19.9 %copy-start.17 = (f32[256,128]{1,0:T(8,128)S(1)}, f32[256,128]{1,0:T(8,128)}, u32[]{:S(2)}) copy-start(f32[256,128]{1,0:T(8,128)} %param.21) | copy-start | bytes 393220
  (54 other events, 187.7 us)
Sparse Core Ops, SparseCore 0:
  60.8 267.1 all-reduce.1
where the time goes:
time: 646 us; the launch traced here: 635 us
  waiting for transfers between devices  257 us (40%)
  matrix products  207 us (32%)
  local copies, waits for them, and re-layouts  101 us (16%)
  other arithmetic  42.9 us (7%)
  between operations  14.2 us (2%)
  starting transfers between devices  12.7 us (2%)
    psum x1, waiting for transfers between devices, shards(): factors = lax.psum(partial_factors, ('gx', 'gy', 'gz'))  253 us
    dot_general x27, matrix products, pair_term(): jnp.einsum('...bij,...bcj->...ci', kernel, weighted, precision=highest)  122 us
    mul x27, local copies, waits for them, and re-layouts, pair_term(): weighted = radial_mix[:, :, None] * nearby[..., None, :channels, :]  49 us
    while x108, local copies, waits for them, and re-layouts  43.9 us
    sqrt x27, other arithmetic, radial_kernel(): distance = jnp.sqrt(squared)  24.8 us
    dot_general x1, matrix products, shards(): imag_part = jnp.einsum('kxyza,xyzca->kc', sine, charges, precision=highest)  21.3 us
    dot_general x1, matrix products, shards(): jnp.einsum('kxyza,xyzca->kc', cosine, charges, precision=highest)  21.1 us
    dot_general x1, matrix products, shards(): second = jnp.einsum('kc,kxyza->xyzca', filtered[1], sine, precision=highest)  19.3 us
  transfers between devices with their start and end apart: 7, of which 2 were waited for; matrix products, arithmetic and copies ran while one was open for 11% of the time, Pallas kernels for 0%

commit v1 on v0

v1 whole, which is shorter than its diff:
```python
import math
import functools
import jax, jax.numpy as jnp, numpy as np
from jax import lax
from jax.experimental import pallas as pl
from jax.experimental.pallas import tpu as pltpu

f32 = jnp.float32
bf16 = jnp.bfloat16
NN = (((1,), (0,)), ((), ()))
NT = (((1,), (1,)), ((), ()))
TN = (((0,), (0,)), ((), ()))
LOG2E = 1.4426950408889634


def split(x):
    hi = x.astype(bf16)
    return hi, (x - hi.astype(f32)).astype(bf16)


def mm(a, b, dims):
    return lax.dot_general(a, b, dims, preferred_element_type=f32)


def mm3(a, b, dims):
    ah, al = split(a)
    bh, bl = split(b)
    return mm(ah, bh, dims) + (mm(ah, bl, dims) + mm(al, bh, dims))


def sincos(u):
    r = u - jnp.round(u)
    z = r * r
    s = jnp.full_like(z, S_C[-1])
    for c in S_C[-2::-1]:
        s = s * z + c
    s = s * r
    c_ = jnp.full_like(z, C_C[-1])
    for c in C_C[-2::-1]:
        c_ = c_ * z + c
    return 1.0 - 2.0 * (s * s), 2.0 * (s * c_)


def fit(fun, deg, lim):
    k = np.arange(200)
    z = 0.5 * lim * (1 - np.cos(np.pi * (k + 0.5) / 200))
    ch = np.polynomial.chebyshev.Chebyshev.fit(z, fun(z), deg, domain=[0, lim])
    return [float(v) for v in ch.convert(kind=np.polynomial.Polynomial).coef]


S_C = fit(lambda z: np.sinc(np.sqrt(z)) * np.pi, 4, 0.25)
C_C = fit(lambda z: np.cos(np.pi * np.sqrt(z)), 5, 0.25)


def phase_operand(pos_ref, cell0):
    rows = []
    for d, n in enumerate((16.0, 8.0, 8.0)):
        parts = []
        for p in range(4):
            off = (p // 2, p % 2, 0)[d]
            parts.append((pos_ref[p, d:d + 1, :] + (cell0[d] + off).astype(f32)) * (1.0 / n))
        v = jnp.concatenate(parts, axis=1)
        a = v.astype(bf16)
        v = v - a.astype(f32)
        b = v.astype(bf16)
        v = v - b.astype(f32)
        rows += [a, b, v.astype(bf16)]
    rows.append(jnp.zeros((7, 512), bf16))
    return jnp.concatenate(rows, axis=0)


def wave_operand(waves_ref, w16_ref):
    w = waves_ref[...].astype(f32)
    w16_ref[...] = jnp.concatenate(
        [w[d:d + 1] for d in range(3) for _ in range(3)] + [jnp.zeros((7, 2048), f32)], axis=0).astype(bf16)


def cell_origin():
    return (lax.axis_index("gx") * 2, lax.axis_index("gy") * 2, lax.axis_index("gz"))


def kernel_a(origin, feat, pos, counts, waves, wv, wc, hout, fout, w16, q2):
    wave_operand(waves, w16)
    lane = lax.broadcasted_iota(jnp.int32, (128, 128), 1)
    sub = lax.broadcasted_iota(jnp.int32, (128, 128), 0)
    for p in range(4):
        f = feat[p]
        n = counts[p]
        v = mm3(f, wv[...], TN)
        hout[p, 0:128, :] = jnp.where(sub < n, v, 0.0)
        hout[p, 128:136, :] = jnp.concatenate([pos[p], jnp.zeros((5, 128), f32)], axis=0)
        q = jnp.where(lane < n, mm3(wc[...], f, TN), 0.0)
        hi, lo = split(q)
        q2[0:128, p * 128:(p + 1) * 128] = hi
        q2[128:256, p * 128:(p + 1) * 128] = lo
    fr = phase_operand(pos, origin())

    def body(kb, _):
        u = mm(w16[:, pl.ds(pl.multiple_of(kb * 256, 256), 256)], fr, TN)
        c, s = sincos(u)
        for t, k in ((c, kb), (s, kb + 8)):
            th, tl = split(t)
            big = mm(q2[...], th, NT)
            fout[k] = big[0:128] + (big[128:256] + mm(q2[0:128], tl, NT))
        return 0
    lax.fori_loop(0, 8, body, 0)


def call_a(origin, feat, pos, counts, waves, wv, wc):
    V = pl.BlockSpec(memory_space=pltpu.VMEM)
    S = pl.BlockSpec(memory_space=pltpu.SMEM)
    return pl.pallas_call(
        functools.partial(kernel_a, origin),
        out_shape=(jax.ShapeDtypeStruct((4, 136, 128), f32), jax.ShapeDtypeStruct((16, 128, 256), f32)),
        in_specs=[V, V, S, V, V, V], out_specs=(V, V),
        scratch_shapes=[pltpu.VMEM((16, 2048), bf16), pltpu.VMEM((256, 512), bf16)],
        name="ka",
    )(feat, pos, counts, waves, wv, wc)


def kernel_c(origin, feat, pos, counts, waves, msg, fil, wh, wo, out, w16):
    wave_operand(waves, w16)
    fr = phase_operand(pos, origin())

    def body(kb, pot):
        u = mm(w16[:, pl.ds(pl.multiple_of(kb * 256, 256), 256)], fr, TN)
        c, s = sincos(u)
        for t, k in ((c, kb), (s, kb + 8)):
            th, tl = split(t)
            gh, gl = split(fil[k])
            big = mm(jnp.concatenate([gh, gl], axis=0), th, NN)
            pot = pot + (big[0:128] + (big[128:256] + mm(gh, tl, NN)))
        return pot
    pot = lax.fori_loop(0, 8, body, jnp.zeros((128, 512), f32))
    lane = lax.broadcasted_iota(jnp.int32, (128, 128), 1)
    for p in range(4):
        mixed = feat[p] + 0.125 * msg[p].T + pot[:, p * 128:(p + 1) * 128]
        h = mm3(wh[...], mixed, TN)
        h = h / (1.0 + jnp.exp(-h))
        o = mixed + mm3(wo[...], h, TN)
        out[p] = jnp.where(lane < counts[p], o, 0.0)


def call_c(origin, feat, pos, counts, waves, msg, fil, wh, wo):
    V = pl.BlockSpec(memory_space=pltpu.VMEM)
    S = pl.BlockSpec(memory_space=pltpu.SMEM)
    return pl.pallas_call(
        functools.partial(kernel_c, origin),
        out_shape=jax.ShapeDtypeStruct((4, 128, 128), f32),
        in_specs=[V, V, S, V, V, V, V, V], out_specs=V,
        scratch_shapes=[pltpu.VMEM((16, 2048), bf16)],
        name="kc",
    )(feat, pos, counts, waves, msg, fil, wh, wo)


IC = 32
SHIFTS = [(a, b, c) for a in range(3) for b in range(3) for c in range(3)]


def own_positions(H, PI, p):
    for d in range(3):
        row = H[1 + p // 2, 1 + p % 2, 1, 128 + d:129 + d, :]
        PI[p, d] = jnp.broadcast_to(row, (128, 128)).T


def make_vb(H, vb, x, y, z):
    hi, lo = split(H[x, y, z, 0:128, :])
    vb[x, y, z, :, 0:128] = hi
    vb[x, y, z, :, 128:256] = lo


def build(H, PI, K, p, px, py, ic, xs):
    i0 = pl.multiple_of(ic * IC, IC)
    own = [PI[p, d, pl.ds(i0, IC), :] for d in range(3)]
    for n, (a, b, c) in enumerate(SHIFTS):
        sft = (a - 1.0, b - 1.0, c - 1.0)
        r2 = None
        for d in range(3):
            row = H[px + a, py + b, c, 128 + d:129 + d, :] + sft[d]
            u = row - own[d]
            r2 = u * u if r2 is None else r2 + u * u
        e = jnp.maximum(1.0 - r2, 0.0)
        e = e * e
        if (a, b, c) == (1, 1, 1):
            ii = lax.broadcasted_iota(jnp.int32, (IC, 128), 0) + i0
            jj = lax.broadcasted_iota(jnp.int32, (IC, 128), 1)
            e = jnp.where(ii == jj, 0.0, e)
        rc = jnp.maximum(r2, 1e-30)
        w = jnp.exp2((rc * lax.rsqrt(rc)) * (14.0 * LOG2E))
        h = jnp.exp2(r2 * (-49.0 * LOG2E)) * e
        for k in range(8):
            hi, lo = split(h)
            K[k * IC:(k + 1) * IC, n * 128:(n + 1) * 128] = hi
            K[(k + 8) * IC:(k + 9) * IC, n * 128:(n + 1) * 128] = lo
            if k < 7:
                h = h * w


def multiply(vb, K, mix_ref, msg, p, px, py, ic):
    acc = None
    for a in range(3):
        v = vb[px + a, pl.ds(py, 3), :, :, :].reshape(1152, 256)
        t = mm(K[:, a * 1152:(a + 1) * 1152], v, NN)
        acc = t if acc is None else acc + t
    out = None
    for k in range(8):
        hh = acc[k * IC:(k + 1) * IC, :]
        t = hh[:, 0:128] + (hh[:, 128:256] + acc[(k + 8) * IC:(k + 9) * IC, 0:128])
        t = t * mix_ref[k:k + 1, :]
        out = t if out is None else out + t
    msg[p, pl.ds(pl.multiple_of(ic * IC, IC), IC), :] = out


def kernel_pairs(H, mix, msg, vb, PI, K, m8):
    for k in range(8):
        m8[k:k + 1, :] = mix[k:k + 1, :] * math.exp(-float(k * k))
    for p in range(4):
        own_positions(H, PI, p)

    def conv(n, _):
        make_vb(H, vb, n // 12, (n // 3) % 4, n % 3)
        return 0
    lax.fori_loop(0, 48, conv, 0)

    def body(t, _):
        p = t // (128 // IC)
        ic = t % (128 // IC)
        build(H, PI, K, p, p // 2, p % 2, ic, None)
        multiply(vb, K, m8, msg, p, p // 2, p % 2, ic)
        return 0
    lax.fori_loop(0, 4 * (128 // IC), body, 0)


def call_pairs(H, mix, kern=kernel_pairs, kslots=1):
    V = pl.BlockSpec(memory_space=pltpu.VMEM)
    return pl.pallas_call(
        kern,
        out_shape=jax.ShapeDtypeStruct((4, 128, 128), f32),
        in_specs=[V, V], out_specs=V,
        scratch_shapes=[pltpu.VMEM((4, 4, 3, 128, 256), bf16), pltpu.VMEM((4, 3, 128, 128), f32)]
        + [pltpu.VMEM((16 * IC, 3456), bf16)] * kslots + [pltpu.VMEM((8, 128), f32)],
        name="kpairs",
    )(H, mix)


MESH_ID = pl.DeviceIdType.MESH
FILTER_SCALE = 1.0 / math.sqrt(131072.0) / math.sqrt(2048.0)


class Place:
    def __init__(self):
        self.gx = lax.axis_index("gx")
        self.gy = lax.axis_index("gy")
        self.gz = lax.axis_index("gz")
        self.core = self.gx % 2
        self.zh = self.gx // 2
        self.x = self.gy
        self.y = self.gz // 2
        self.zl = self.gz % 2
        self.z = self.zh * 2 + self.zl

    def at_gx(self, v):
        return (v, self.gy, self.gz)

    def at_gy(self, v):
        return (self.gx, v, self.gz)

    def at_gz(self, v):
        return (self.gx, self.gy, v)

    def at_y(self, v):
        return (self.gx, self.gy, v * 2 + self.zl)

    def at_z(self, v):
        return (v // 2 * 2 + self.core, self.gy, self.y * 2 + v % 2)


def flip(v, bits):
    if bits == 1:
        return v + 1 - 2 * (v % 2)
    if bits == 3:
        return 3 - v
    return (v + 2) % 4


class Copies:
    def __init__(self, send, recv):
        self.send, self.recv, self.n, self.started = send, recv, 0, []

    def start(self, src, dst, device):
        i = self.n
        self.n += 1
        cp = pltpu.make_async_remote_copy(
            src_ref=src, dst_ref=dst, send_sem=self.send.at[i], recv_sem=self.recv.at[i],
            device_id=device, device_id_type=MESH_ID)
        cp.start()
        self.started.append(cp)
        return cp

    def finish(self):
        for cp in self.started:
            cp.wait_send()


def enter(me):
    bar = pltpu.get_barrier_semaphore()
    peers = [me.at_gx((me.gx + 1) % 8), me.at_gx((me.gx + 7) % 8),
             me.at_gy((me.gy + 1) % 4), me.at_gy((me.gy + 3) % 4),
             me.at_gz((me.gz + 2) % 8), me.at_gz((me.gz + 6) % 8)]
    peers += [me.at_z((me.z + i) % 8) for i in range(1, 8)]
    for p in peers:
        pl.semaphore_signal(bar, inc=1, device_id=p, device_id_type=MESH_ID)
    pl.semaphore_wait(bar, len(peers))


def halo_steps(me, cp, H):
    st = {}

    def h0():
        st["pair"] = cp.start(H.at[1:3, 1:3, 1], H.at[1:3, 1:3, 2 * me.zl], me.at_gz(me.gz + 1 - 2 * me.zl))

    def h1():
        st["pair"].wait_recv()
        st["fwd"] = cp.start(H.at[1:3, 1:3, 2 - 2 * me.zl], H.at[1:3, 1:3, 2 * me.zl],
                             me.at_gz((me.gz + 2 + 4 * me.zl) % 8))

    def h2():
        st["fwd"].wait_recv()
        up, down = me.at_gx((me.gx + 1) % 8), me.at_gx((me.gx + 7) % 8)
        st["gx"] = [cp.start(H.at[2, 1:3], H.at[0, 1:3], up), cp.start(H.at[1, 1:3], H.at[3, 1:3], down)]
        up, down = me.at_gy((me.gy + 1) % 4), me.at_gy((me.gy + 3) % 4)
        st["gy"] = [cp.start(H.at[1:3, 2], H.at[1:3, 0], up), cp.start(H.at[1:3, 1], H.at[1:3, 3], down)]

    def h3():
        for c in st["gx"]:
            c.wait_recv()
        up, down = me.at_gy((me.gy + 1) % 4), me.at_gy((me.gy + 3) % 4)
        for col in (0, 3):
            st["gy"].append(cp.start(H.at[col, 2], H.at[col, 0], up))
            st["gy"].append(cp.start(H.at[col, 1], H.at[col, 3], down))

    def h4():
        for c in st["gy"]:
            c.wait_recv()
    return [h0, h1, h2, h3, h4]


def reduce_steps(me, cp, F, G, R, filt):
    RD, R1, R2, R3, R4, RZ = R
    c64 = me.core * 64
    other = me.at_gx(me.gx + 1 - 2 * me.core)
    st = {}
    groups = []
    for g in range(4):
        bits = (1, 3) if g % 2 == 0 else (3, 1)
        rows = pl.ds(pl.multiple_of(c64 + 16 * g, 16), 16)
        axes = [(me.y, me.at_y), (me.x, me.at_gy)]
        if g >= 2:
            axes = axes[::-1]

        def view(ref, first, second, rows=rows, g=g):
            return ref.at[first, second, rows] if g < 2 else ref.at[second, first, rows]
        groups.append((g, bits, rows, axes, view))
    ALL = slice(None)

    def r0():
        for g in range(4):
            rows = pl.ds(pl.multiple_of(64 - c64 + 16 * g, 16), 16)
            st["D", g] = cp.start(F.at[:, :, rows], RD.at[g], other)

    def r1():
        for g, bits, rows, axes, view in groups:
            st["D", g].wait_recv()
            F[:, :, rows] = F[:, :, rows] + RD[g]
            v, at = axes[0]
            dev = at(flip(v, bits[0]))
            st["1", g] = [cp.start(view(F, flip(v, bits[0]), ALL), R1.at[g, 0], dev),
                          cp.start(view(F, flip(v, 2), ALL), R1.at[g, 1], dev)]

    def add(ref, first, second, val, g, rows):
        if g < 2:
            ref[first, second, rows] = ref[first, second, rows] + val
        else:
            ref[second, first, rows] = ref[second, first, rows] + val

    def r2():
        for g, bits, rows, axes, view in groups:
            v, at = axes[0]
            keep = (v, flip(v, bits[1]))
            for i in (1, 0):
                st["1", g][i].wait_recv()
                add(F, keep[i], ALL, R1[g, i], g, rows)
            st["2", g] = cp.start(view(F, keep[1], ALL), R2.at[g], at(flip(v, bits[1])))

    def r3():
        for g, bits, rows, axes, view in groups:
            v, at = axes[0]
            st["2", g].wait_recv()
            add(F, v, ALL, R2[g], g, rows)
            u, at = axes[1]
            dev = at(flip(u, bits[0]))
            st["3", g] = [cp.start(view(F, v, flip(u, bits[0])), R3.at[g, 0], dev),
                          cp.start(view(F, v, flip(u, 2)), R3.at[g, 1], dev)]

    def r4():
        for g, bits, rows, axes, view in groups:
            v = axes[0][0]
            u, at = axes[1]
            keep = (u, flip(u, bits[1]))
            for i in (1, 0):
                st["3", g][i].wait_recv()
                add(F, v, keep[i], R3[g, i], g, rows)
            st["4", g] = cp.start(view(F, v, keep[1]), R4.at[g], at(flip(u, bits[1])))

    def zrows(z):
        return pl.ds(pl.multiple_of(c64 + 8 * z, 8), 8)

    def r5():
        for g, bits, rows, axes, view in groups:
            st["4", g].wait_recv()
            add(F, axes[0][0], axes[1][0], R4[g], g, rows)
        for i in range(1, 8):
            z = (me.z + i) % 8
            st["z", i] = cp.start(F.at[me.y, me.x, zrows(z)], RZ.at[i], me.at_z(z))

    def r6():
        total = F[me.y, me.x, zrows(me.z)]
        for i in range(1, 8):
            st["z", i].wait_recv()
            total = total + RZ[i]
        G[me.y, me.x, zrows(me.z)] = total * filt()
        for i in range(1, 8):
            mine = G.at[me.y, me.x, zrows(me.z)]
            st["Z", i] = cp.start(mine, mine, me.at_z((me.z + i) % 8))

    def same(ref, dev):
        return cp.start(ref, ref, dev)

    def r7():
        for i in range(1, 8):
            st["Z", i].wait_recv()
        for g, bits, rows, axes, view in groups:
            v = axes[0][0]
            u, at = axes[1]
            st["4b", g] = same(view(G, v, u), at(flip(u, bits[1])))

    def r8():
        for g, bits, rows, axes, view in groups:
            v = axes[0][0]
            u, at = axes[1]
            st["4b", g].wait_recv()
            dev = at(flip(u, bits[0]))
            st["3b", g] = [same(view(G, v, u), dev), same(view(G, v, flip(u, bits[1])), dev)]

    def r9():
        for g, bits, rows, axes, view in groups:
            v, at = axes[0]
            for c in st["3b", g]:
                c.wait_recv()
            st["2b", g] = same(view(G, v, ALL), at(flip(v, bits[1])))

    def r10():
        for g, bits, rows, axes, view in groups:
            v, at = axes[0]
            st["2b", g].wait_recv()
            dev = at(flip(v, bits[0]))
            st["1b", g] = [same(view(G, v, ALL), dev), same(view(G, flip(v, bits[1]), ALL), dev)]

    def r11():
        for g, bits, rows, axes, view in groups:
            for c in st["1b", g]:
                c.wait_recv()
            st["Db", g] = same(G.at[:, :, rows], other)

    def r12():
        for g in range(4):
            st["Db", g].wait_recv()
    return [r0, r1, r2, r3, r4, r5, r6, r7, r8, r9, r10, r11, r12]


def kernel_b(hin, fin, filt_hbm, mix, msg, G, H, F, RD, R1, R2, R3, R4, RZ, fbuf, ftr, vb, PI, K, m8, send, recv, lsem):
    me = Place()
    kb = me.y * 4 + me.x
    local = [pltpu.make_async_copy(fin, F, lsem.at[0]),
             pltpu.make_async_copy(filt_hbm.at[pl.ds(pl.multiple_of((kb % 8) * 256, 256), 256)], fbuf, lsem.at[1])]
    local += [pltpu.make_async_copy(hin.at[p], H.at[1 + p // 2, 1 + p % 2, 1], lsem.at[2 + p]) for p in range(4)]
    for c in local:
        c.start()
    enter(me)
    for c in local:
        c.wait()
    cp = Copies(send, recv)

    def filt():
        ftr[...] = fbuf[...].T
        return ftr[pl.ds(pl.multiple_of(me.core * 64 + 8 * me.z, 8), 8), :] * FILTER_SCALE

    hs = halo_steps(me, cp, H)
    rs = reduce_steps(me, cp, F, G, (RD, R1, R2, R3, R4, RZ), filt)
    hs[0]()
    rs[0]()
    for k in range(8):
        m8[k:k + 1, :] = mix[k:k + 1, :] * math.exp(-float(k * k))
    for p in range(4):
        own_positions(H, PI, p)
    hs[1]()
    rs[1]()
    hs[2]()
    rs[2]()
    hs[3]()
    rs[3]()
    rs[4]()
    hs[4]()
    rs[5]()

    def conv(n, _):
        make_vb(H, vb, n // 12, (n // 3) % 4, n % 3)
        return 0
    lax.fori_loop(0, 48, conv, 0)
    rs[6]()

    def body(t, _):
        p = t // (128 // IC)
        ic = t % (128 // IC)
        build(H, PI, K, p, p // 2, p % 2, ic, None)
        multiply(vb, K, m8, msg, p, p // 2, p % 2, ic)
        return 0
    done = 0
    for step, until in zip(rs[7:], (2, 4, 6, 8, 11, 16)):
        lax.fori_loop(done, until, body, 0)
        done = until
        step()
    cp.finish()


NCOPY = 88


def call_b(hout, fout, filt, mix):
    V = pl.BlockSpec(memory_space=pltpu.VMEM)
    A = pl.BlockSpec(memory_space=pl.ANY)
    return pl.pallas_call(
        kernel_b,
        out_shape=(jax.ShapeDtypeStruct((4, 128, 128), f32), jax.ShapeDtypeStruct((4, 4, 128, 256), f32)),
        in_specs=[A, A, A, V], out_specs=(V, V),
        scratch_shapes=[
            pltpu.VMEM((4, 4, 3, 136, 128), f32), pltpu.VMEM((4, 4, 128, 256), f32),
            pltpu.VMEM((4, 4, 4, 16, 256), f32), pltpu.VMEM((4, 2, 4, 16, 256), f32),
            pltpu.VMEM((4, 4, 16, 256), f32), pltpu.VMEM((4, 2, 16, 256), f32),
            pltpu.VMEM((4, 16, 256), f32), pltpu.VMEM((8, 8, 256), f32),
            pltpu.VMEM((256, 128), f32), pltpu.VMEM((128, 256), f32),
            pltpu.VMEM((4, 4, 3, 128, 256), bf16), pltpu.VMEM((4, 3, 128, 128), f32),
            pltpu.VMEM((16 * IC, 3456), bf16), pltpu.VMEM((8, 128), f32),
            pltpu.SemaphoreType.DMA((NCOPY,)), pltpu.SemaphoreType.DMA((NCOPY,)), pltpu.SemaphoreType.DMA((6,)),
        ],
        compiler_params=pltpu.CompilerParams(collective_id=0, has_side_effects=True),
        name="kb",
    )(hout, fout.reshape(4, 4, 128, 256), filt, mix)


def shards(features, positions, counts, waves, filter_table, w_value, w_charge, radial_mix, w_hidden, w_out):
    feat = features.reshape(4, 128, 128)
    pos = positions.reshape(4, 3, 128)
    cnt = counts.reshape(4)
    hout, fout = call_a(cell_origin, feat, pos, cnt, waves, w_value, w_charge)
    msg, fil = call_b(hout, fout, filter_table, radial_mix)
    out = call_c(cell_origin, feat, pos, cnt, waves, msg, fil.reshape(16, 128, 256), w_hidden, w_out)
    return out.reshape(features.shape)


def solution(mesh):
    from jax.sharding import PartitionSpec as P
    cell = P("gx", "gy", "gz")
    five = P("gx", "gy", "gz", None, None)
    return jax.shard_map(
        shards, mesh=mesh,
        in_specs=(five, five, cell) + (P(),) * 7,
        out_specs=five, check_vma=False)
```

time: 646 us -> 108 us (0.17); the launches traced: 635 us -> 107 us
  waiting for transfers between devices: 257 us -> 0 us
  matrix products: 207 us -> 0 us
  Pallas kernels: 0 us -> 103 us
  local copies, waits for them, and re-layouts: 101 us -> 2.46 us
  other arithmetic: 42.9 us -> 1.34 us
  between operations: 14.2 us -> 0.01 us
  starting transfers between devices: 12.7 us -> 0 us
    psum x1 -> x0, waiting for transfers between devices: 253 us -> none  [shards(): factors = lax.psum(partial_factors, ('gx', 'gy', 'gz'))]
    dot_general x35 -> x0, matrix products: 207 us -> none  [the longest x27 122 us: pair_term(): jnp.einsum('...bij,...bcj->...ci', kernel, weighted, precision=highest)]
    pallas_call x0 -> x3, Pallas kernels: none -> 103 us  [the longest x1 80.5 us: call_b(): pl.pallas_call(kernel_b, out_shape=(jax.ShapeDtypeStruct((4, 128, 128), f...]
    mul x28 -> x0, local copies, waits for them, and re-layouts: 49.8 us -> none  [the longest x27 49 us: pair_term(): weighted = radial_mix[:, :, None] * nearby[..., None, :channels, :]]
    while x109 -> x0, local copies, waits for them, and re-layouts: 45 us -> none
    sqrt x27 -> x0, other arithmetic: 24.8 us -> none  [radial_kernel(): distance = jnp.sqrt(squared)]
    ppermute x6 -> x0, starting transfers between devices: 12.7 us -> none  [the longest x3 8.22 us: with_halo(): lax.ppermute(lax.slice_in_dim(block, block.shape[dim] - width, None, axis...]
    reduce_sum x27 -> x0, other arithmetic: 7.33 us -> none  [radial_kernel(): squared = jnp.sum(offsets * offsets, axis=-3)]
  transfers between devices with their start and end apart: 7 -> 0, of which waited for: 2 -> 0; matrix products, arithmetic and copies ran while one was open for 11% -> 0% of each run, Pallas kernels for 0% -> 0%
where the time goes in v1:
time: 108 us; the launch traced here: 107 us
  Pallas kernels  103 us (95%)
  local copies, waits for them, and re-layouts  2.46 us (2%)
  other arithmetic  1.34 us (1%)
    pallas_call x1, Pallas kernels, call_b(): pl.pallas_call(kernel_b, out_shape=(jax.ShapeDtypeStruct((4, 128, 128), f...  80.5 us
    pallas_call x1, Pallas kernels, call_c(): pl.pallas_call(functools.partial(kernel_c, origin), out_shape=jax.ShapeDt...  11.9 us
    pallas_call x1, Pallas kernels, call_a(): pl.pallas_call(functools.partial(kernel_a, origin), out_shape=(jax.ShapeD...  10.6 us

profile of v1, /device:TPU:1, one launch (start us, length us, event | category | flops | bytes accessed | tf_op | source)
XLA Modules:
  0.0 106.8 jit_solution(12377147930730584994)
XLA Ops:
  0.0 0.5 broadcast.3
  0.5 1.3 %reduce.3 = s32[2,2]{1,0:T(2,128)S(1)} reduce(s32[2,2,1]{1,2,0:T(1,128)} %param.12, s32[]{:T(128)} %broadcast.3), dimensions={2}, to_apply=%param.12.reduce_sub_computation.3 | reduce | bytes 36 | tf_op args[2]
  1.9 0.7 reshape.20.counts
  2.5 0.7 copy.12
  3.2 0.6 copy.14.pos
  3.8 10.6 %ka.1 = (f32[4,136,128]{2,1,0:T(8,128)}, f32[16,128,256]{2,1,0:T(8,128)}) custom-call(f32[4,128,128]{2,1,0:T(8,128)} %bitcast.10, f32[4,3,128]{2,1,0:T(4,128)} %copy.14.pos, s32[4]{0:T(128)} %reshape.20.counts, s32[3,2048]{1,0:T(4,128)} %waves.3, f32[128,128]{1,0:T(8,128)} %wv.1, f32[128,128]{1,0:T(8,128)} %wc.1), custom_call_target="tpu_custom_call" | custom-call | tf_op jit(solution)/shard_map/ka/pallas_call | solution.py:112
  14.4 80.5 %kb.1 = (f32[4,128,128]{2,1,0:T(8,128)}, f32[4,4,128,256]{3,2,1,0:T(8,128)}) custom-call(f32[4,136,128]{2,1,0:T(8,128)} %get-tuple-element.9.hin, f32[4,4,128,256]{3,2,1,0:T(8,128)} %bitcast.9, f32[2048,128]{1,0:T(8,128)} %filt_hbm.1, f32[8,128]{1,0:T(8,128)} %mix.1), custom_call_target="tpu_custom_call" | custom-call | tf_op jit(solution)/shard_map/kb/pallas_call | solution.py:542
  94.9 11.9 %kc.1 = f32[4,128,128]{2,1,0:T(8,128)} custom-call(f32[4,128,128]{2,1,0:T(8,128)} %bitcast.11, f32[4,3,128]{2,1,0:T(4,128)} %copy.14.pos, s32[4]{0:T(128)} %reshape.20.counts, s32[3,2048]{1,0:T(4,128)} %waves.3, f32[4,128,128]{2,1,0:T(8,128)} %get-tuple-element.11.msg, f32[16,128,256]{2,1,0:T(8,128)} %bitcast.8, f32[128,256]{1,0:T(8,128)} %wh.1, f32[256,128]{1,0:T(8,128)} %wo.1), custom_call_target="tpu_custom_call" | custom-call | tf_op jit(solution)/shard_map/kc/pallas_call | solution.py:147

commit v2 on v1

v2 whole, which is shorter than its diff:
```python
import math
import functools
import jax, jax.numpy as jnp, numpy as np
from jax import lax
from jax.experimental import pallas as pl
from jax.experimental.pallas import tpu as pltpu
from jax.sharding import PartitionSpec as P

f32 = jnp.float32
bf16 = jnp.bfloat16
NN = (((1,), (0,)), ((), ()))
NT = (((1,), (1,)), ((), ()))
TN = (((0,), (0,)), ((), ()))
LOG2E = 1.4426950408889634
ALL = slice(None)


def split(x):
    hi = x.astype(bf16)
    return hi, (x - hi.astype(f32)).astype(bf16)


def mm(a, b, dims):
    return lax.dot_general(a, b, dims, preferred_element_type=f32)


def mm3(a, b, dims):
    ah, al = split(a)
    bh, bl = split(b)
    return mm(ah, bh, dims) + (mm(ah, bl, dims) + mm(al, bh, dims))


def fit(fun, deg, lim):
    k = np.arange(200)
    z = 0.5 * lim * (1 - np.cos(np.pi * (k + 0.5) / 200))
    ch = np.polynomial.chebyshev.Chebyshev.fit(z, fun(z), deg, domain=[0, lim])
    return [float(v) for v in ch.convert(kind=np.polynomial.Polynomial).coef]


S_C = fit(lambda z: math.sqrt(2.0) * np.sinc(np.sqrt(z)) * np.pi, 4, 0.25)
C_C = fit(lambda z: math.sqrt(2.0) * np.cos(np.pi * np.sqrt(z)), 4, 0.25)


def sincos(u):
    r = u - jnp.round(u)
    z = r * r
    s = S_C[3] + S_C[4] * z
    c = C_C[3] + C_C[4] * z
    for i in (2, 1, 0):
        s = s * z + S_C[i]
        c = c * z + C_C[i]
    s = s * r
    return 1.0 - s * s, s * c


def phase_operand(pos, cell0):
    rows = []
    for d, n in enumerate((16.0, 8.0, 8.0)):
        parts = []
        for p in range(4):
            off = (p // 2, p % 2, 0)[d]
            parts.append((pos[p // 2, p % 2, d] + (cell0[d] + off).astype(f32)) * (1.0 / n))
        v = jnp.concatenate(parts, axis=1)
        a = v.astype(bf16)
        v = v - a.astype(f32)
        b = v.astype(bf16)
        v = v - b.astype(f32)
        rows += [a, b, v.astype(bf16)]
    rows.append(jnp.zeros((7, 512), bf16))
    return jnp.concatenate(rows, axis=0)


def wave_operand(waves, w16):
    w = waves[...].astype(f32)
    w16[...] = jnp.concatenate(
        [w[d:d + 1] for d in range(3) for _ in range(3)] + [jnp.zeros((7, 2048), f32)], axis=0).astype(bf16)


IC = 32


def own_positions(H, PI, p):
    for d in range(3):
        row = H[1 + p // 2, 1 + p % 2, 1, 128 + d:129 + d, :]
        PI[p, d] = jnp.broadcast_to(row, (128, 128)).T


def make_vb(H, vb, x, y, z):
    hi, lo = split(H[x, y, z, 0:128, :])
    vb[x, y, z, :, 0:128] = hi
    vb[x, y, z, :, 128:256] = lo


def build(H, own, K, n, cell, shift, i0, is_self):
    x, y, z = cell
    r2 = None
    for d in range(3):
        row = H[x, y, z, 128 + d:129 + d, :] + shift[d]
        u = row - own[d]
        r2 = u * u if r2 is None else r2 + u * u
    e = jnp.maximum(1.0 - r2, 0.0)
    e = e * e
    if is_self is not None:
        ii = lax.broadcasted_iota(jnp.int32, (IC, 128), 0) + (i0 + jnp.where(is_self, 0, 1024))
        jj = lax.broadcasted_iota(jnp.int32, (IC, 128), 1)
        e = jnp.where(ii == jj, 0.0, e)
    rc = jnp.maximum(r2, 1e-30)
    w = jnp.exp2((rc * lax.rsqrt(rc)) * (14.0 * LOG2E))
    h = jnp.exp2(r2 * (-49.0 * LOG2E)) * e
    cols = slice(n * 128, (n + 1) * 128)
    for k in range(8):
        hi, lo = split(h)
        K[k * IC:(k + 1) * IC, cols] = hi
        K[(k + 8) * IC:(k + 9) * IC, cols] = lo
        if k < 7:
            h = h * w


def pair_unit(H, PI, vb, K, mix, msg, t, phase):
    p = t // (128 // IC)
    ic = t % (128 // IC)
    px, py = p // 2, p % 2
    i0 = pl.multiple_of(ic * IC, IC)
    own = [PI[p, d, pl.ds(i0, IC), :] for d in range(3)]
    if phase == 0:
        runs = [[(x, y, z) for y in (1, 2) for z in range(3)] for x in (1, 2)]
    elif phase == 1:
        runs = [[(x, 3 * py, z) for z in range(3)] for x in (1, 2)]
    else:
        runs = [[(3 * px, py + b, z) for b in range(3) for z in range(3)]]
    n = 0
    acc = None
    for run in runs:
        first = n
        for cell in run:
            x, y, z = cell
            shift = [jnp.asarray(x - 1 - px).astype(f32), jnp.asarray(y - 1 - py).astype(f32), z - 1.0]
            is_self = (p == (x - 1) * 2 + (y - 1)) if phase == 0 and z == 1 else None
            build(H, own, K, n, cell, shift, i0, is_self)
            n += 1
        x, y, _ = run[0]
        v = vb[x, pl.ds(y, len(run) // 3)].reshape(128 * len(run), 256)
        t_ = mm(K[:, first * 128:n * 128], v, NN)
        acc = t_ if acc is None else acc + t_
    out = None
    for k in range(8):
        hh = acc[k * IC:(k + 1) * IC, :]
        s = (hh[:, 0:128] + (hh[:, 128:256] + acc[(k + 8) * IC:(k + 9) * IC, 0:128])) * mix[k:k + 1, :]
        out = s if out is None else out + s
    rows = pl.ds(i0, IC)
    if phase == 0:
        msg[p, rows, :] = out
    else:
        msg[p, rows, :] = msg[p, rows, :] + out


MESH_ID = pl.DeviceIdType.MESH
FILTER_SCALE = 1.0 / math.sqrt(131072.0) / math.sqrt(2048.0)


class Place:
    def __init__(self):
        self.gx = lax.axis_index("gx")
        self.gy = lax.axis_index("gy")
        self.gz = lax.axis_index("gz")
        self.core = self.gx % 2
        self.zh = self.gx // 2
        self.x = self.gy
        self.y = self.gz // 2
        self.zl = self.gz % 2
        self.z = self.zh * 2 + self.zl

    def at_gx(self, v):
        return (v, self.gy, self.gz)

    def at_gy(self, v):
        return (self.gx, v, self.gz)

    def at_gz(self, v):
        return (self.gx, self.gy, v)

    def at_y(self, v):
        return (self.gx, self.gy, v * 2 + self.zl)

    def at_z(self, v):
        return (v // 2 * 2 + self.core, self.gy, self.y * 2 + v % 2)


def flip(v, bits):
    if bits == 1:
        return v + 1 - 2 * (v % 2)
    if bits == 3:
        return 3 - v
    return (v + 2) % 4


class Copies:
    def __init__(self, send, recv):
        self.send, self.recv, self.n, self.started = send, recv, 0, []

    def start(self, src, dst, device):
        i = self.n
        self.n += 1
        cp = pltpu.make_async_remote_copy(
            src_ref=src, dst_ref=dst, send_sem=self.send.at[i], recv_sem=self.recv.at[i],
            device_id=device, device_id_type=MESH_ID)
        cp.start()
        self.started.append(cp)
        return cp

    def finish(self):
        for cp in self.started:
            cp.wait_send()


def greet(me):
    bar = pltpu.get_barrier_semaphore()
    peers = [me.at_gx((me.gx + 1) % 8), me.at_gx((me.gx + 7) % 8),
             me.at_gy((me.gy + 1) % 4), me.at_gy((me.gy + 3) % 4),
             me.at_gz((me.gz + 2) % 8), me.at_gz((me.gz + 6) % 8)]
    peers += [me.at_z((me.z + i) % 8) for i in range(1, 8)]
    for p in peers:
        pl.semaphore_signal(bar, inc=1, device_id=p, device_id_type=MESH_ID)
    return lambda: pl.semaphore_wait(bar, len(peers))


def halo_steps(me, cp, H):
    st = {}
    up_y, down_y = me.at_gy((me.gy + 1) % 4), me.at_gy((me.gy + 3) % 4)
    up_x, down_x = me.at_gx((me.gx + 1) % 8), me.at_gx((me.gx + 7) % 8)

    def h0():
        st["pair"] = [cp.start(H.at[1 + p // 2, 1 + p % 2, 1], H.at[1 + p // 2, 1 + p % 2, 2 * me.zl],
                               me.at_gz(me.gz + 1 - 2 * me.zl)) for p in range(4)]
        st["gy"] = [cp.start(H.at[1:3, 2, 1], H.at[1:3, 0, 1], up_y),
                    cp.start(H.at[1:3, 1, 1], H.at[1:3, 3, 1], down_y)]

    def h1():
        st["fwd"] = []
        for p in range(4):
            st["pair"][p].wait_recv()
            c = (1 + p // 2, 1 + p % 2)
            st["fwd"].append(cp.start(H.at[c[0], c[1], 2 - 2 * me.zl], H.at[c[0], c[1], 2 * me.zl],
                                      me.at_gz((me.gz + 2 + 4 * me.zl) % 8)))

    def h2():
        for c in st["fwd"]:
            c.wait_recv()
        for z in (0, 2):
            st["gy"].append(cp.start(H.at[1:3, 2, z], H.at[1:3, 0, z], up_y))
            st["gy"].append(cp.start(H.at[1:3, 1, z], H.at[1:3, 3, z], down_y))
        st["gx"] = [cp.start(H.at[2, 1:3], H.at[0, 1:3], up_x), cp.start(H.at[1, 1:3], H.at[3, 1:3], down_x)]

    def h3():
        for c in st["gy"]:
            c.wait_recv()
        for y in (0, 3):
            st["gx"].append(cp.start(H.at[2, y], H.at[0, y], up_x))
            st["gx"].append(cp.start(H.at[1, y], H.at[3, y], down_x))

    def h4():
        for c in st["gx"]:
            c.wait_recv()
    return [h0, h1, h2, h3, h4]


def core_copy(me, F, RD, dsem, i):
    rows = pl.ds(pl.multiple_of(64 - me.core * 64, 64), 64)
    return pltpu.make_async_remote_copy(
        src_ref=F.at[i // 4, i % 4, :, rows], dst_ref=RD.at[i // 4, i % 4],
        send_sem=dsem.at[0, i], recv_sem=dsem.at[1, i],
        device_id=me.at_gx(me.gx + 1 - 2 * me.core), device_id_type=MESH_ID)


def reduce_steps(me, cp, Fs, Gs, Rs, dsem, filt, h):
    F, G = Fs.at[h], Gs.at[h]
    RD, R1, R2, R3, R4, RZ = [r.at[h] for r in Rs]
    c64 = me.core * 64
    other = me.at_gx(me.gx + 1 - 2 * me.core)
    st = {}
    groups = []
    for g in range(4):
        bits = (1, 3) if g % 2 == 0 else (3, 1)
        rows = pl.ds(pl.multiple_of(c64 + 16 * g, 16), 16)
        axes = [(me.y, me.at_y), (me.x, me.at_gy)]
        if g >= 2:
            axes = axes[::-1]

        def view(ref, first, second, rows=rows, g=g):
            return ref.at[first, second, rows] if g < 2 else ref.at[second, first, rows]
        groups.append((g, bits, rows, axes, view))

    def r1():
        for i in range(4 * h, 4 * h + 4):
            core_copy(me, Fs, Rs[0], dsem, i).wait_recv()
        for g, bits, rows, axes, view in groups:
            F[:, :, rows] = F[:, :, rows] + RD[:, :, 16 * g:16 * g + 16]
            v, at = axes[0]
            dev = at(flip(v, bits[0]))
            st["1", g] = [cp.start(view(F, flip(v, bits[0]), ALL), R1.at[g, 0], dev),
                          cp.start(view(F, flip(v, 2), ALL), R1.at[g, 1], dev)]

    def add(ref, first, second, val, g, rows):
        if g < 2:
            ref[first, second, rows] = ref[first, second, rows] + val
        else:
            ref[second, first, rows] = ref[second, first, rows] + val

    def r2():
        for g, bits, rows, axes, view in groups:
            v, at = axes[0]
            keep = (v, flip(v, bits[1]))
            for i in (1, 0):
                st["1", g][i].wait_recv()
                add(F, keep[i], ALL, R1[g, i], g, rows)
            st["2", g] = cp.start(view(F, keep[1], ALL), R2.at[g], at(flip(v, bits[1])))

    def r3():
        for g, bits, rows, axes, view in groups:
            v, at = axes[0]
            st["2", g].wait_recv()
            add(F, v, ALL, R2[g], g, rows)
            u, at = axes[1]
            dev = at(flip(u, bits[0]))
            st["3", g] = [cp.start(view(F, v, flip(u, bits[0])), R3.at[g, 0], dev),
                          cp.start(view(F, v, flip(u, 2)), R3.at[g, 1], dev)]

    def r4():
        for g, bits, rows, axes, view in groups:
            v = axes[0][0]
            u, at = axes[1]
            keep = (u, flip(u, bits[1]))
            for i in (1, 0):
                st["3", g][i].wait_recv()
                add(F, v, keep[i], R3[g, i], g, rows)
            st["4", g] = cp.start(view(F, v, keep[1]), R4.at[g], at(flip(u, bits[1])))

    def zrows(z):
        return pl.ds(pl.multiple_of(c64 + 8 * z, 8), 8)

    def r5():
        for g, bits, rows, axes, view in groups:
            st["4", g].wait_recv()
            add(F, axes[0][0], axes[1][0], R4[g], g, rows)
        for i in (4, 3, 5, 2, 6, 1, 7):
            z = (me.z + i) % 8
            st["z", i] = cp.start(F.at[me.y, me.x, zrows(z)], RZ.at[i], me.at_z(z))

    def r6():
        total = F[me.y, me.x, zrows(me.z)]
        for i in (1, 7, 2, 6, 3, 5, 4):
            st["z", i].wait_recv()
            total = total + RZ[i]
        G[me.y, me.x, zrows(me.z)] = total * filt()
        for i in (4, 3, 5, 2, 6, 1, 7):
            mine = G.at[me.y, me.x, zrows(me.z)]
            st["Z", i] = cp.start(mine, mine, me.at_z((me.z + i) % 8))

    def same(ref, dev):
        return cp.start(ref, ref, dev)

    def r7():
        for i in range(1, 8):
            st["Z", i].wait_recv()
        for g, bits, rows, axes, view in groups:
            v = axes[0][0]
            u, at = axes[1]
            st["4b", g] = same(view(G, v, u), at(flip(u, bits[1])))

    def r8():
        for g, bits, rows, axes, view in groups:
            v = axes[0][0]
            u, at = axes[1]
            st["4b", g].wait_recv()
            dev = at(flip(u, bits[0]))
            st["3b", g] = [same(view(G, v, u), dev), same(view(G, v, flip(u, bits[1])), dev)]

    def r9():
        for g, bits, rows, axes, view in groups:
            v, at = axes[0]
            for c in st["3b", g]:
                c.wait_recv()
            st["2b", g] = same(view(G, v, ALL), at(flip(v, bits[1])))

    def r10():
        st["Db"] = []
        for g, bits, rows, axes, view in groups:
            v, at = axes[0]
            st["2b", g].wait_recv()
            dev = at(flip(v, bits[0]))
            st["1b", g] = [same(view(G, v, ALL), dev), same(view(G, flip(v, bits[1]), ALL), dev)]
        for g, bits, rows, axes, view in groups:
            v = axes[0][0]
            for s in (v, flip(v, bits[1])):
                st["Db"].append(same(view(G, s, ALL), other))

    def r11():
        for g, bits, rows, axes, view in groups:
            v = axes[0][0]
            for c in st["1b", g]:
                c.wait_recv()
            for s in (flip(v, bits[0]), flip(v, 2)):
                st["Db"].append(same(view(G, s, ALL), other))

    def r12():
        for c in st["Db"]:
            c.wait_recv()
    return [None, r1, r2, r3, r4, r5, r6, r7, r8, r9, r10, r11, r12]


PLAN = [
    ("factors", 4, 6), ("r", 0, 1), ("factors", 6, 8), ("r", 1, 1), ("h", 1), ("r", 0, 2), ("h", 2), ("cA",), ("r", 1, 2), ("A", 2),
    ("r", 0, 3), ("A", 2), ("r", 1, 3), ("A", 2), ("r", 0, 4), ("A", 2), ("r", 1, 4), ("A", 1), ("r", 0, 5), ("A", 2), ("r", 1, 5),
    ("A", 3), ("h", 3), ("r", 0, 6), ("A", 2), ("r", 1, 6), ("cB",), ("B", 4), ("r", 0, 7), ("B", 4), ("r", 1, 7), ("B", 4),
    ("r", 0, 8), ("B", 4), ("r", 1, 8), ("h", 4), ("cC",), ("r", 0, 9), ("C", 3), ("r", 1, 9), ("C", 3), ("r", 0, 10), ("C", 3),
    ("r", 1, 10), ("C", 3), ("r", 0, 11), ("C", 4), ("r", 1, 11), ("r", 0, 12), ("pot", 0), ("r", 1, 12), ("pot", 1),
]


def kernel(feat, pos, counts, waves, filt_hbm, wv, wc, mix, wh, wo, out,
           H, F, G, RD, R1, R2, R3, R4, RZ, TH, TL, q2, w16, fbuf, ftr, vb, PI, K, m8, msg, potr,
           send, recv, dsem, lsem):
    me = Place()
    fcopy = [pltpu.make_async_copy(
        filt_hbm.at[pl.ds(pl.multiple_of((4 * h + me.y) * 256 + (me.x % 2) * 128, 128), 128)], fbuf.at[h], lsem.at[h])
        for h in range(2)]
    for c in fcopy:
        c.start()
    greeted = greet(me)
    lane = lax.broadcasted_iota(jnp.int32, (128, 128), 1)
    sub = lax.broadcasted_iota(jnp.int32, (128, 128), 0)
    cells = [(p // 2, p % 2, 0) for p in range(4)]
    for p, c in enumerate(cells):
        q = jnp.where(lane < counts[c[0], 0, c[1]], mm3(wc[...], feat[c], TN), 0.0)
        hi, lo = split(q)
        q2[0:128, p * 128:(p + 1) * 128] = hi
        q2[128:256, p * 128:(p + 1) * 128] = lo
        v = mm3(feat[c], wv[...], TN)
        H[1 + c[0], 1 + c[1], 1, 0:128, :] = jnp.where(sub < counts[c[0], 0, c[1]], v, 0.0)
        H[1 + c[0], 1 + c[1], 1, 128:136, :] = jnp.concatenate(
            [pos[c[0], c[1], d] for d in range(3)] + [jnp.zeros((5, 128), f32)], axis=0)
    wave_operand(waves, w16)
    fr = phase_operand(pos, (me.gx * 2, me.gy * 2, me.gz))

    def factors(i, send_now):
        u = mm(w16[:, pl.ds(pl.multiple_of(i * 256, 256), 256)], fr, TN)
        c, s = sincos(u)
        for t, k, x in ((c, i, 0), (s, i + 8, 2)):
            th, tl = split(t)
            TH[k] = th
            TL[k] = tl
            big = mm(q2[...], th, NT)
            f = big[0:128] + (big[128:256] + mm(q2[0:128], tl, NT))
            F[i // 4, i % 4, x] = f[:, 0:128]
            F[i // 4, i % 4, x + 1] = f[:, 128:256]
        if send_now:
            core_copy(me, F, RD, dsem, i).start()

    def factor_loop(lo, hi, send_now):
        def body(i, _):
            factors(i, send_now)
            return 0
        lax.fori_loop(lo, hi, body, 0)
    factor_loop(0, 4, False)
    for c in fcopy:
        c.wait()
    for h in range(2):
        ftr[h] = fbuf[h].T
    for k in range(8):
        m8[k:k + 1, :] = mix[k:k + 1, :] * math.exp(-float(k * k))
    for p in range(4):
        own_positions(H, PI, p)
    greeted()
    for i in range(4):
        core_copy(me, F, RD, dsem, i).start()
    cp = Copies(send, recv)
    hs = halo_steps(me, cp, H)
    hs[0]()

    def filt(h):
        return lambda: ftr[h, pl.ds(pl.multiple_of(me.core * 64 + 8 * me.z, 8), 8), :] * FILTER_SCALE

    rs = [reduce_steps(me, cp, F, G, (RD, R1, R2, R3, R4, RZ), dsem, filt(h), h) for h in range(2)]

    def convert(cells_of, n):
        def body(i, _):
            make_vb(H, vb, *cells_of(i))
            return 0
        lax.fori_loop(0, n, body, 0)

    def potential(h):
        def body(j, acc):
            y, t = j // 2, j % 2
            g = jnp.concatenate([G[h, y, 2 * t], G[h, y, 2 * t + 1]], axis=1)
            gh, gl = split(g)
            k = 4 * h + y + 8 * t
            big = mm(jnp.concatenate([gh, gl], axis=0), TH[k], NN)
            return acc + (big[0:128] + (big[128:256] + mm(gh, TL[k], NN)))
        potr[...] = lax.fori_loop(0, 8, body, potr[...] if h else jnp.zeros((128, 512), f32))

    at = {"A": 0, "B": 0, "C": 0}
    for item in PLAN:
        if item[0] == "h":
            hs[item[1]]()
        elif item[0] == "r":
            rs[item[1]][item[2]]()
        elif item[0] == "factors":
            factor_loop(item[1], item[2], True)
        elif item[0] == "pot":
            potential(item[1])
        elif item[0] == "cA":
            convert(lambda i: (1 + i // 6, 1 + (i // 3) % 2, i % 3), 12)
        elif item[0] == "cB":
            convert(lambda i: (1 + i // 6, 3 * ((i // 3) % 2), i % 3), 12)
        elif item[0] == "cC":
            convert(lambda i: (3 * (i // 12), (i // 3) % 4, i % 3), 24)
        else:
            def body(t, _, phase="ABC".index(item[0])):
                pair_unit(H, PI, vb, K, m8, msg, t, phase)
                return 0
            lax.fori_loop(at[item[0]], at[item[0]] + item[1], body, 0)
            at[item[0]] += item[1]
    assert all(v in (0, 16) for v in at.values())

    for p, c in enumerate(cells):
        mixed = feat[c] + 0.125 * msg[p].T + potr[:, p * 128:(p + 1) * 128]
        h = mm3(wh[...], mixed, TN)
        h = h / (1.0 + jnp.exp(-h))
        o = mixed + mm3(wo[...], h, TN)
        out[c] = jnp.where(lane < counts[c[0], 0, c[1]], o, 0.0)
    cp.finish()
    for i in range(8):
        core_copy(me, F, RD, dsem, i).wait_send()


NCOPY = 176


def shards(features, positions, counts, waves, filter_table, w_value, w_charge, radial_mix, w_hidden, w_out):
    V = pl.BlockSpec(memory_space=pltpu.VMEM)
    S = pl.BlockSpec(memory_space=pltpu.SMEM)
    A = pl.BlockSpec(memory_space=pl.ANY)
    vm = pltpu.VMEM
    return pl.pallas_call(
        kernel,
        out_shape=jax.ShapeDtypeStruct(features.shape, f32),
        in_specs=[V, V, S, V, A, V, V, V, V, V], out_specs=V,
        scratch_shapes=[
            vm((4, 4, 3, 136, 128), f32), vm((2, 4, 4, 128, 128), f32), vm((2, 4, 4, 128, 128), f32),
            vm((2, 4, 4, 64, 128), f32), vm((2, 4, 2, 4, 16, 128), f32),
            vm((2, 4, 4, 16, 128), f32), vm((2, 4, 2, 16, 128), f32),
            vm((2, 4, 16, 128), f32), vm((2, 8, 8, 128), f32),
            vm((16, 256, 512), bf16), vm((16, 256, 512), bf16), vm((256, 512), bf16), vm((16, 2048), bf16),
            vm((2, 128, 128), f32), vm((2, 128, 128), f32),
            vm((4, 4, 3, 128, 256), bf16), vm((4, 3, 128, 128), f32),
            vm((16 * IC, 1536), bf16), vm((8, 128), f32), vm((4, 128, 128), f32), vm((128, 512), f32),
            pltpu.SemaphoreType.DMA((NCOPY,)), pltpu.SemaphoreType.DMA((NCOPY,)),
            pltpu.SemaphoreType.DMA((2, 8)), pltpu.SemaphoreType.DMA((2,)),
        ],
        compiler_params=pltpu.CompilerParams(collective_id=0, has_side_effects=True),
        name="layer",
    )(features, positions.reshape(2, 2, 3, 1, 128), counts.reshape(2, 1, 2), waves, filter_table,
      w_value, w_charge, radial_mix, w_hidden, w_out)


def solution(mesh):
    cell = P("gx", "gy", "gz")
    five = P("gx", "gy", "gz", None, None)
    return jax.shard_map(
        shards, mesh=mesh,
        in_specs=(five, five, cell) + (P(),) * 7,
        out_specs=five, check_vma=False)
```

time: 108 us -> 87.3 us (0.81)
  Pallas kernels: 103 us -> 84.9 us
  other arithmetic: 1.34 us -> 0 us
    pallas_call x3 -> x1, Pallas kernels: 103 us -> 84.9 us  [shards(): pl.pallas_call(kernel, out_shape=jax.ShapeDtypeStruct(features.shape, f32...]
    unnamed x1 -> x0, other arithmetic: 1.34 us -> none
    reshape x2 -> x0, local copies, waits for them, and re-layouts: 1.25 us -> none  [the longest x1 0.65 us: shards(): cnt = counts.reshape(4)]
where the time goes in v2:
time: 87.3 us; the launch traced here: 86.6 us
  Pallas kernels  84.9 us (97%)
  local copies, waits for them, and re-layouts  1.67 us (2%)
    pallas_call x1, Pallas kernels, shards(): pl.pallas_call(kernel, out_shape=jax.ShapeDtypeStruct(features.shape, f32...  84.9 us

profile of v2, /device:TPU:1, one launch (start us, length us, event | category | flops | bytes accessed | tf_op | source)
XLA Modules:
  0.0 86.6 jit_solution(9834586662166847309)
XLA Ops:
  0.0 84.9 %layer.1 = f32[2,2,1,128,128]{4,3,2,1,0:T(8,128)} custom-call(f32[2,2,1,128,128]{4,3,2,1,0:T(8,128)} %feat.1, f32[2,2,3,1,128]{4,3,2,1,0:T(1,128)} %bitcast.4, s32[2,1,2]{2,1,0:T(1,128)} %bitcast.5, s32[3,2048]{1,0:T(4,128)} %waves.1, f32[2048,128]{1,0:T(8,128)} %filt_hbm.1, f32[128,128]{1,0:T(8,128)} %wv.1, f32[128,128]{1,0:T(8,128)} %wc.1, f32[8,128]{1,0:T(8,128)} %mix.1, ...), custom_call_target="tpu_custom_call" | custom-call | tf_op jit(solution)/shard_map/layer/pallas_call | solution.py:544
  84.9 1.7 %copy.13 = f32[2,2,1,128,128]{4,3,2,1,0:T(8,128)} copy(f32[2,2,1,128,128]{4,3,2,1,0:T(8,128)} %layer.1) | data formatting | bytes 524288

commit v3 on v2

--- a/solution.py
+++ b/solution.py
@@ -85,10 +85,13 @@
         PI[p, d] = jnp.broadcast_to(row, (128, 128)).T
 
 
-def make_vb(H, vb, x, y, z):
+OWN_CELLS = [(x, y, 1) for x in (1, 2) for y in (1, 2)] + [(x, y, z) for x in (1, 2) for y in (1, 2) for z in (0, 2)]
+
+
+def make_vb(H, dst, at, x, y, z):
     hi, lo = split(H[x, y, z, 0:128, :])
-    vb[x, y, z, :, 0:128] = hi
-    vb[x, y, z, :, 128:256] = lo
+    dst[at + (ALL, slice(0, 128))] = hi
+    dst[at + (ALL, slice(128, 256))] = lo
 
 
 def build(H, own, K, n, cell, shift, i0, is_self):
@@ -116,15 +119,17 @@
             h = h * w
 
 
-def pair_unit(H, PI, vb, K, mix, msg, t, phase):
+def pair_unit(H, PI, va, vb, K, mix, msg, t, phase):
     p = t // (128 // IC)
     ic = t % (128 // IC)
     px, py = p // 2, p % 2
     i0 = pl.multiple_of(ic * IC, IC)
     own = [PI[p, d, pl.ds(i0, IC), :] for d in range(3)]
     if phase == 0:
-        runs = [[(x, y, z) for y in (1, 2) for z in range(3)] for x in (1, 2)]
+        runs = [OWN_CELLS[0:4]]
     elif phase == 1:
+        runs = [OWN_CELLS[4:12]]
+    elif phase == 2:
         runs = [[(x, 3 * py, z) for z in range(3)] for x in (1, 2)]
     else:
         runs = [[(3 * px, py + b, z) for b in range(3) for z in range(3)]]
@@ -135,11 +140,14 @@
         for cell in run:
             x, y, z = cell
             shift = [jnp.asarray(x - 1 - px).astype(f32), jnp.asarray(y - 1 - py).astype(f32), z - 1.0]
-            is_self = (p == (x - 1) * 2 + (y - 1)) if phase == 0 and z == 1 else None
+            is_self = (p == (x - 1) * 2 + (y - 1)) if phase == 0 else None
             build(H, own, K, n, cell, shift, i0, is_self)
             n += 1
         x, y, _ = run[0]
-        v = vb[x, pl.ds(y, len(run) // 3)].reshape(128 * len(run), 256)
+        if phase < 2:
+            v = va[4 * phase:4 * phase + len(run)].reshape(128 * len(run), 256)
+        else:
+            v = vb[x, pl.ds(y, len(run) // 3)].reshape(128 * len(run), 256)
         t_ = mm(K[:, first * 128:n * 128], v, NN)
         acc = t_ if acc is None else acc + t_
     out = None
@@ -217,7 +225,8 @@
     bar = pltpu.get_barrier_semaphore()
     peers = [me.at_gx((me.gx + 1) % 8), me.at_gx((me.gx + 7) % 8),
              me.at_gy((me.gy + 1) % 4), me.at_gy((me.gy + 3) % 4),
-             me.at_gz((me.gz + 2) % 8), me.at_gz((me.gz + 6) % 8)]
+             me.at_gz((me.gz + 2) % 8), me.at_gz((me.gz + 6) % 8),
+             me.at_gy((me.gy + 2) % 4), me.at_gz((me.gz + 4) % 8)]
     peers += [me.at_z((me.z + i) % 8) for i in range(1, 8)]
     for p in peers:
         pl.semaphore_signal(bar, inc=1, device_id=p, device_id_type=MESH_ID)
@@ -246,22 +255,30 @@
     def h2():
         for c in st["fwd"]:
             c.wait_recv()
+        st["gx"] = [cp.start(H.at[1 + me.core, 1:3], H.at[3 - 3 * me.core, 1:3], me.at_gx((me.gx + 7 + 2 * me.core) % 8)),
+                    cp.start(H.at[2 - me.core, 1:3], H.at[3 * me.core, 1:3], me.at_gx(me.gx + 1 - 2 * me.core))]
+
+    def h3():
         for z in (0, 2):
             st["gy"].append(cp.start(H.at[1:3, 2, z], H.at[1:3, 0, z], up_y))
             st["gy"].append(cp.start(H.at[1:3, 1, z], H.at[1:3, 3, z], down_y))
-        st["gx"] = [cp.start(H.at[2, 1:3], H.at[0, 1:3], up_x), cp.start(H.at[1, 1:3], H.at[3, 1:3], down_x)]
-
-    def h3():
+
+    def h4():
+        for c in st["gx"]:
+            c.wait_recv()
+        far = 3 * me.core
+        st["corner"] = [cp.start(H.at[far, 2], H.at[far, 0], up_y), cp.start(H.at[far, 1], H.at[far, 3], down_y)]
+
+    def h5():
         for c in st["gy"]:
             c.wait_recv()
         for y in (0, 3):
-            st["gx"].append(cp.start(H.at[2, y], H.at[0, y], up_x))
-            st["gx"].append(cp.start(H.at[1, y], H.at[3, y], down_x))
-
-    def h4():
-        for c in st["gx"]:
+            st["corner"].append(cp.start(H.at[2 - me.core, y], H.at[3 * me.core, y], me.at_gx(me.gx + 1 - 2 * me.core)))
+
+    def h6():
+        for c in st["corner"]:
             c.wait_recv()
-    return [h0, h1, h2, h3, h4]
+    return [h0, h1, h2, h3, h4, h5, h6]
 
 
 def core_copy(me, F, RD, dsem, i):
@@ -274,7 +291,7 @@
 
 def reduce_steps(me, cp, Fs, Gs, Rs, dsem, filt, h):
     F, G = Fs.at[h], Gs.at[h]
-    RD, R1, R2, R3, R4, RZ = [r.at[h] for r in Rs]
+    RD, R1, R2, R3, RZ = [r.at[h] for r in Rs]
     c64 = me.core * 64
     other = me.at_gx(me.gx + 1 - 2 * me.core)
     st = {}
@@ -321,32 +338,21 @@
             st["2", g].wait_recv()
             add(F, v, ALL, R2[g], g, rows)
             u, at = axes[1]
-            dev = at(flip(u, bits[0]))
-            st["3", g] = [cp.start(view(F, v, flip(u, bits[0])), R3.at[g, 0], dev),
-                          cp.start(view(F, v, flip(u, 2)), R3.at[g, 1], dev)]
-
-    def r4():
-        for g, bits, rows, axes, view in groups:
-            v = axes[0][0]
-            u, at = axes[1]
-            keep = (u, flip(u, bits[1]))
-            for i in (1, 0):
-                st["3", g][i].wait_recv()
-                add(F, v, keep[i], R3[g, i], g, rows)
-            st["4", g] = cp.start(view(F, v, keep[1]), R4.at[g], at(flip(u, bits[1])))
+            st["3", g] = [cp.start(view(F, v, (u + i) % 4), R3.at[g, i - 1], at((u + i) % 4)) for i in (2, 1, 3)]
 
     def zrows(z):
         return pl.ds(pl.multiple_of(c64 + 8 * z, 8), 8)
 
-    def r5():
-        for g, bits, rows, axes, view in groups:
-            st["4", g].wait_recv()
-            add(F, axes[0][0], axes[1][0], R4[g], g, rows)
+    def r4():
+        for g, bits, rows, axes, view in groups:
+            for c in st["3", g]:
+                c.wait_recv()
+            add(F, axes[0][0], axes[1][0], R3[g, 0] + (R3[g, 1] + R3[g, 2]), g, rows)
         for i in (4, 3, 5, 2, 6, 1, 7):
             z = (me.z + i) % 8
             st["z", i] = cp.start(F.at[me.y, me.x, zrows(z)], RZ.at[i], me.at_z(z))
 
-    def r6():
+    def r5():
         total = F[me.y, me.x, zrows(me.z)]
         for i in (1, 7, 2, 6, 3, 5, 4):
             st["z", i].wait_recv()
@@ -359,30 +365,21 @@
     def same(ref, dev):
         return cp.start(ref, ref, dev)
 
-    def r7():
+    def r6():
         for i in range(1, 8):
             st["Z", i].wait_recv()
         for g, bits, rows, axes, view in groups:
-            v = axes[0][0]
             u, at = axes[1]
-            st["4b", g] = same(view(G, v, u), at(flip(u, bits[1])))
-
-    def r8():
-        for g, bits, rows, axes, view in groups:
-            v = axes[0][0]
-            u, at = axes[1]
-            st["4b", g].wait_recv()
-            dev = at(flip(u, bits[0]))
-            st["3b", g] = [same(view(G, v, u), dev), same(view(G, v, flip(u, bits[1])), dev)]
-
-    def r9():
+            st["3b", g] = [same(view(G, axes[0][0], u), at((u + i) % 4)) for i in (2, 1, 3)]
+
+    def r7():
         for g, bits, rows, axes, view in groups:
             v, at = axes[0]
             for c in st["3b", g]:
                 c.wait_recv()
             st["2b", g] = same(view(G, v, ALL), at(flip(v, bits[1])))
 
-    def r10():
+    def r8():
         st["Db"] = []
         for g, bits, rows, axes, view in groups:
             v, at = axes[0]
@@ -394,7 +391,7 @@
             for s in (v, flip(v, bits[1])):
                 st["Db"].append(same(view(G, s, ALL), other))
 
-    def r11():
+    def r9():
         for g, bits, rows, axes, view in groups:
             v = axes[0][0]
             for c in st["1b", g]:
@@ -402,23 +399,39 @@
             for s in (flip(v, bits[0]), flip(v, 2)):
                 st["Db"].append(same(view(G, s, ALL), other))
 
-    def r12():
+    def r10():
         for c in st["Db"]:
             c.wait_recv()
-    return [None, r1, r2, r3, r4, r5, r6, r7, r8, r9, r10, r11, r12]
-
-
-PLAN = [
-    ("factors", 4, 6), ("r", 0, 1), ("factors", 6, 8), ("r", 1, 1), ("h", 1), ("r", 0, 2), ("h", 2), ("cA",), ("r", 1, 2), ("A", 2),
-    ("r", 0, 3), ("A", 2), ("r", 1, 3), ("A", 2), ("r", 0, 4), ("A", 2), ("r", 1, 4), ("A", 1), ("r", 0, 5), ("A", 2), ("r", 1, 5),
-    ("A", 3), ("h", 3), ("r", 0, 6), ("A", 2), ("r", 1, 6), ("cB",), ("B", 4), ("r", 0, 7), ("B", 4), ("r", 1, 7), ("B", 4),
-    ("r", 0, 8), ("B", 4), ("r", 1, 8), ("h", 4), ("cC",), ("r", 0, 9), ("C", 3), ("r", 1, 9), ("C", 3), ("r", 0, 10), ("C", 3),
-    ("r", 1, 10), ("C", 3), ("r", 0, 11), ("C", 4), ("r", 1, 11), ("r", 0, 12), ("pot", 0), ("r", 1, 12), ("pot", 1),
+    return [None, r1, r2, r3, r4, r5, r6, r7, r8, r9, r10]
+
+
+EVENTS = [
+    "f46", "r01", "f68", "r11", "ca", "a4", "h1", "r02", "a4", "r12", "a4", "h2", "cA", "r03", "A1", "r13",
+    "a4", "r04", "h3", "A3", "r14", "A4", "r05", "h4", "A3", "r15", "A3", "r06", "h5", "cB", "A2", "r16",
+    "B4", "r07", "B4", "r17", "B4", "r08", "B4", "r18", "h6", "cC", "C3", "r09", "C3", "r19", "C3", "r010",
+    "p0", "C3", "r110", "C4", "p1",
 ]
 
 
+def parse(events):
+    for w in events:
+        if w[0] == "r":
+            yield "r", int(w[1]), int(w[2:])
+        elif w[0] == "f":
+            yield "factors", int(w[1]), int(w[2])
+        elif w[0] == "p":
+            yield "pot", int(w[1])
+        elif w[0] == "c":
+            yield (w,)
+        else:
+            yield {"h": "h", "a": 0, "A": 1, "B": 2, "C": 3}[w[0]], int(w[1:])
+
+
+PLAN = list(parse(EVENTS))
+
+
 def kernel(feat, pos, counts, waves, filt_hbm, wv, wc, mix, wh, wo, out,
-           H, F, G, RD, R1, R2, R3, R4, RZ, TH, TL, q2, w16, fbuf, ftr, vb, PI, K, m8, msg, potr,
+           H, F, G, RD, R1, R2, R3, RZ, TH, TL, q2, w16, fbuf, ftr, va, vb, PI, K, m8, msg, potr,
            send, recv, dsem, lsem):
     me = Place()
     fcopy = [pltpu.make_async_copy(
@@ -480,11 +493,12 @@
     def filt(h):
         return lambda: ftr[h, pl.ds(pl.multiple_of(me.core * 64 + 8 * me.z, 8), 8), :] * FILTER_SCALE
 
-    rs = [reduce_steps(me, cp, F, G, (RD, R1, R2, R3, R4, RZ), dsem, filt(h), h) for h in range(2)]
+    rs = [reduce_steps(me, cp, F, G, (RD, R1, R2, R3, RZ), dsem, filt(h), h) for h in range(2)]
 
     def convert(cells_of, n):
         def body(i, _):
-            make_vb(H, vb, *cells_of(i))
+            c = cells_of(i)
+            make_vb(H, vb, c, *c)
             return 0
         lax.fori_loop(0, n, body, 0)
 
@@ -498,7 +512,7 @@
             return acc + (big[0:128] + (big[128:256] + mm(gh, TL[k], NN)))
         potr[...] = lax.fori_loop(0, 8, body, potr[...] if h else jnp.zeros((128, 512), f32))
 
-    at = {"A": 0, "B": 0, "C": 0}
+    at = [0, 0, 0, 0]
     for item in PLAN:
         if item[0] == "h":
             hs[item[1]]()
@@ -508,19 +522,22 @@
             factor_loop(item[1], item[2], True)
         elif item[0] == "pot":
             potential(item[1])
+        elif item[0] == "ca":
+            for n in range(4):
+                make_vb(H, va, (n,), *OWN_CELLS[n])
         elif item[0] == "cA":
-            convert(lambda i: (1 + i // 6, 1 + (i // 3) % 2, i % 3), 12)
+            for n in range(4, 12):
+                make_vb(H, va, (n,), *OWN_CELLS[n])
         elif item[0] == "cB":
             convert(lambda i: (1 + i // 6, 3 * ((i // 3) % 2), i % 3), 12)
         elif item[0] == "cC":
             convert(lambda i: (3 * (i // 12), (i // 3) % 4, i % 3), 24)
         else:
-            def body(t, _, phase="ABC".index(item[0])):
-                pair_unit(H, PI, vb, K, m8, msg, t, phase)
+            def body(t, _, phase=item[0]):
+                pair_unit(H, PI, va, vb, K, m8, msg, t, phase)
                 return 0
             lax.fori_loop(at[item[0]], at[item[0]] + item[1], body, 0)
             at[item[0]] += item[1]
-    assert all(v in (0, 16) for v in at.values())
 
     for p, c in enumerate(cells):
         mixed = feat[c] + 0.125 * msg[p].T + potr[:, p * 128:(p + 1) * 128]
@@ -548,12 +565,12 @@
         scratch_shapes=[
             vm((4, 4, 3, 136, 128), f32), vm((2, 4, 4, 128, 128), f32), vm((2, 4, 4, 128, 128), f32),
             vm((2, 4, 4, 64, 128), f32), vm((2, 4, 2, 4, 16, 128), f32),
-            vm((2, 4, 4, 16, 128), f32), vm((2, 4, 2, 16, 128), f32),
-            vm((2, 4, 16, 128), f32), vm((2, 8, 8, 128), f32),
+            vm((2, 4, 4, 16, 128), f32), vm((2, 4, 3, 16, 128), f32),
+            vm((2, 8, 8, 128), f32),
             vm((16, 256, 512), bf16), vm((16, 256, 512), bf16), vm((256, 512), bf16), vm((16, 2048), bf16),
             vm((2, 128, 128), f32), vm((2, 128, 128), f32),
-            vm((4, 4, 3, 128, 256), bf16), vm((4, 3, 128, 128), f32),
-            vm((16 * IC, 1536), bf16), vm((8, 128), f32), vm((4, 128, 128), f32), vm((128, 512), f32),
+            vm((12, 128, 256), bf16), vm((4, 4, 3, 128, 256), bf16), vm((4, 3, 128, 128), f32),
+            vm((16 * IC, 1152), bf16), vm((8, 128), f32), vm((4, 128, 128), f32), vm((128, 512), f32),
             pltpu.SemaphoreType.DMA((NCOPY,)), pltpu.SemaphoreType.DMA((NCOPY,)),
             pltpu.SemaphoreType.DMA((2, 8)), pltpu.SemaphoreType.DMA((2,)),
         ],

time: 87.3 us -> 77.1 us (0.88)
  Pallas kernels: 84.9 us -> 75.3 us
    pallas_call x1, Pallas kernels: 84.9 us -> 75.3 us  [shards(): pl.pallas_call(kernel, out_shape=jax.ShapeDtypeStruct(features.shape, f32...]
where the time goes in v3:
time: 77.1 us; the launch traced here: 77 us
  Pallas kernels  75.3 us (98%)
  local copies, waits for them, and re-layouts  1.67 us (2%)
    pallas_call x1, Pallas kernels, shards(): pl.pallas_call(kernel, out_shape=jax.ShapeDtypeStruct(features.shape, f32...  75.3 us
    unnamed x1, local copies, waits for them, and re-layouts  1.67 us

profile of v3, /device:TPU:1, one launch (start us, length us, event | category | flops | bytes accessed | tf_op | source)
XLA Modules:
  0.0 77.0 jit_solution(15618335814852504024)
XLA Ops:
  0.0 75.3 %layer.1 = f32[2,2,1,128,128]{4,3,2,1,0:T(8,128)} custom-call(f32[2,2,1,128,128]{4,3,2,1,0:T(8,128)} %feat.1, f32[2,2,3,1,128]{4,3,2,1,0:T(1,128)} %bitcast.4, s32[2,1,2]{2,1,0:T(1,128)} %bitcast.5, s32[3,2048]{1,0:T(4,128)} %waves.1, f32[2048,128]{1,0:T(8,128)} %filt_hbm.1, f32[128,128]{1,0:T(8,128)} %wv.1, f32[128,128]{1,0:T(8,128)} %wc.1, f32[8,128]{1,0:T(8,128)} %mix.1, ...), custom_call_target="tpu_custom_call" | custom-call | tf_op jit(solution)/shard_map/layer/pallas_call | solution.py:561
  75.3 1.7 %copy.13 = f32[2,2,1,128,128]{4,3,2,1,0:T(8,128)} copy(f32[2,2,1,128,128]{4,3,2,1,0:T(8,128)} %layer.1) | data formatting | bytes 524288

commit v4 on v3

--- a/solution.py
+++ b/solution.py
@@ -119,7 +119,7 @@
             h = h * w
 
 
-def pair_unit(H, PI, va, vb, K, mix, msg, t, phase):
+def pair_unit(H, PI, va, vy, vb, K, mix, msg, t, phase):
     p = t // (128 // IC)
     ic = t % (128 // IC)
     px, py = p // 2, p % 2
@@ -130,7 +130,7 @@
     elif phase == 1:
         runs = [OWN_CELLS[4:12]]
     elif phase == 2:
-        runs = [[(x, 3 * py, z) for z in range(3)] for x in (1, 2)]
+        runs = [[(x, 3 * py, z) for x in (1, 2) for z in range(3)]]
     else:
         runs = [[(3 * px, py + b, z) for b in range(3) for z in range(3)]]
     n = 0
@@ -146,8 +146,10 @@
         x, y, _ = run[0]
         if phase < 2:
             v = va[4 * phase:4 * phase + len(run)].reshape(128 * len(run), 256)
+        elif phase == 2:
+            v = vy[py].reshape(768, 256)
         else:
-            v = vb[x, pl.ds(y, len(run) // 3)].reshape(128 * len(run), 256)
+            v = vb[px, pl.ds(y, 3)].reshape(1152, 256)
         t_ = mm(K[:, first * 128:n * 128], v, NN)
         acc = t_ if acc is None else acc + t_
     out = None
@@ -407,9 +409,9 @@
 
 EVENTS = [
     "f46", "r01", "f68", "r11", "ca", "a4", "h1", "r02", "a4", "r12", "a4", "h2", "cA", "r03", "A1", "r13",
-    "a4", "r04", "h3", "A3", "r14", "A4", "r05", "h4", "A3", "r15", "A3", "r06", "h5", "cB", "A2", "r16",
-    "B4", "r07", "B4", "r17", "B4", "r08", "B4", "r18", "h6", "cC", "C3", "r09", "C3", "r19", "C3", "r010",
-    "p0", "C3", "r110", "C4", "p1",
+    "h3", "a4", "r04", "A3", "r14", "A3", "h4", "r05", "A4", "h5", "cB", "B1", "r15", "A3", "B3", "r06", "B4",
+    "A2", "r16", "B4", "r07", "h6", "cC", "B4", "r17", "C3", "r08", "C3", "r18", "C3", "r09", "C3", "r19",
+    "C3", "r010", "p0", "C1", "r110", "p1",
 ]
 
 
@@ -431,7 +433,7 @@
 
 
 def kernel(feat, pos, counts, waves, filt_hbm, wv, wc, mix, wh, wo, out,
-           H, F, G, RD, R1, R2, R3, RZ, TH, TL, q2, w16, fbuf, ftr, va, vb, PI, K, m8, msg, potr,
+           H, F, G, RD, R1, R2, R3, RZ, TH, TL, q2, w16, fbuf, ftr, va, vy, vb, PI, K, m8, msg, potr,
            send, recv, dsem, lsem):
     me = Place()
     fcopy = [pltpu.make_async_copy(
@@ -495,10 +497,9 @@
 
     rs = [reduce_steps(me, cp, F, G, (RD, R1, R2, R3, RZ), dsem, filt(h), h) for h in range(2)]
 
-    def convert(cells_of, n):
+    def convert(dst, at_of, cells_of, n):
         def body(i, _):
-            c = cells_of(i)
-            make_vb(H, vb, c, *c)
+            make_vb(H, dst, at_of(i), *cells_of(i))
             return 0
         lax.fori_loop(0, n, body, 0)
 
@@ -529,12 +530,12 @@
             for n in range(4, 12):
                 make_vb(H, va, (n,), *OWN_CELLS[n])
         elif item[0] == "cB":
-            convert(lambda i: (1 + i // 6, 3 * ((i // 3) % 2), i % 3), 12)
+            convert(vy, lambda i: (i // 6, (i // 3) % 2, i % 3), lambda i: (1 + (i // 3) % 2, 3 * (i // 6), i % 3), 12)
         elif item[0] == "cC":
-            convert(lambda i: (3 * (i // 12), (i // 3) % 4, i % 3), 24)
+            convert(vb, lambda i: (i // 12, (i // 3) % 4, i % 3), lambda i: (3 * (i // 12), (i // 3) % 4, i % 3), 24)
         else:
             def body(t, _, phase=item[0]):
-                pair_unit(H, PI, va, vb, K, m8, msg, t, phase)
+                pair_unit(H, PI, va, vy, vb, K, m8, msg, t, phase)
                 return 0
             lax.fori_loop(at[item[0]], at[item[0]] + item[1], body, 0)
             at[item[0]] += item[1]
@@ -569,7 +570,7 @@
             vm((2, 8, 8, 128), f32),
             vm((16, 256, 512), bf16), vm((16, 256, 512), bf16), vm((256, 512), bf16), vm((16, 2048), bf16),
             vm((2, 128, 128), f32), vm((2, 128, 128), f32),
-            vm((12, 128, 256), bf16), vm((4, 4, 3, 128, 256), bf16), vm((4, 3, 128, 128), f32),
+            vm((12, 128, 256), bf16), vm((2, 2, 3, 128, 256), bf16), vm((2, 4, 3, 128, 256), bf16), vm((4, 3, 128, 128), f32),
             vm((16 * IC, 1152), bf16), vm((8, 128), f32), vm((4, 128, 128), f32), vm((128, 512), f32),
             pltpu.SemaphoreType.DMA((NCOPY,)), pltpu.SemaphoreType.DMA((NCOPY,)),
             pltpu.SemaphoreType.DMA((2, 8)), pltpu.SemaphoreType.DMA((2,)),

time: 77.1 us -> 76.1 us (0.987)
  Pallas kernels: 75.3 us -> 74.3 us
    pallas_call x1, Pallas kernels: 75.3 us -> 74.3 us  [shards(): pl.pallas_call(kernel, out_shape=jax.ShapeDtypeStruct(features.shape, f32...]
where the time goes in v4:
time: 76.1 us; the launch traced here: 76 us
  Pallas kernels  74.3 us (98%)
  local copies, waits for them, and re-layouts  1.67 us (2%)
    pallas_call x1, Pallas kernels, shards(): pl.pallas_call(kernel, out_shape=jax.ShapeDtypeStruct(features.shape, f32...  74.3 us
    unnamed x1, local copies, waits for them, and re-layouts  1.67 us

profile of v4, /device:TPU:1, one launch (start us, length us, event | category | flops | bytes accessed | tf_op | source)
XLA Modules:
  0.0 76.0 jit_solution(17995298746524368037)
XLA Ops:
  0.0 74.3 %layer.1 = f32[2,2,1,128,128]{4,3,2,1,0:T(8,128)} custom-call(f32[2,2,1,128,128]{4,3,2,1,0:T(8,128)} %feat.1, f32[2,2,3,1,128]{4,3,2,1,0:T(1,128)} %bitcast.4, s32[2,1,2]{2,1,0:T(1,128)} %bitcast.5, s32[3,2048]{1,0:T(4,128)} %waves.1, f32[2048,128]{1,0:T(8,128)} %filt_hbm.1, f32[128,128]{1,0:T(8,128)} %wv.1, f32[128,128]{1,0:T(8,128)} %wc.1, f32[8,128]{1,0:T(8,128)} %mix.1, ...), custom_call_target="tpu_custom_call" | custom-call | tf_op jit(solution)/shard_map/layer/pallas_call | solution.py:562
  74.3 1.7 %copy.13 = f32[2,2,1,128,128]{4,3,2,1,0:T(8,128)} copy(f32[2,2,1,128,128]{4,3,2,1,0:T(8,128)} %layer.1) | data formatting | bytes 524288

commit v5 on v4

--- a/solution.py
+++ b/solution.py
@@ -410,8 +410,8 @@
 EVENTS = [
     "f46", "r01", "f68", "r11", "ca", "a4", "h1", "r02", "a4", "r12", "a4", "h2", "cA", "r03", "A1", "r13",
     "h3", "a4", "r04", "A3", "r14", "A3", "h4", "r05", "A4", "h5", "cB", "B1", "r15", "A3", "B3", "r06", "B4",
-    "A2", "r16", "B4", "r07", "h6", "cC", "B4", "r17", "C3", "r08", "C3", "r18", "C3", "r09", "C3", "r19",
-    "C3", "r010", "p0", "C1", "r110", "p1",
+    "A2", "r16", "B4", "r07", "h6", "cC", "B4", "r17", "C4", "r08", "C3", "r18", "C3", "r09", "C3", "r19",
+    "C3", "r010", "p0", "r110", "p1",
 ]
 
 

time: 76.1 us -> 76.1 us (level)
  no operation moved by 1% of the time
where the time goes in v5:
time: 76.1 us; the launch traced here: 76 us
  Pallas kernels  74.3 us (98%)
  local copies, waits for them, and re-layouts  1.67 us (2%)
    pallas_call x1, Pallas kernels, shards(): pl.pallas_call(kernel, out_shape=jax.ShapeDtypeStruct(features.shape, f32...  74.3 us
    unnamed x1, local copies, waits for them, and re-layouts  1.67 us

profile of v5, /device:TPU:1, one launch (start us, length us, event | category | flops | bytes accessed | tf_op | source)
XLA Modules:
  0.0 76.0 jit_solution(12508772608937534070)
XLA Ops:
  0.0 74.3 %layer.1 = f32[2,2,1,128,128]{4,3,2,1,0:T(8,128)} custom-call(f32[2,2,1,128,128]{4,3,2,1,0:T(8,128)} %feat.1, f32[2,2,3,1,128]{4,3,2,1,0:T(1,128)} %bitcast.4, s32[2,1,2]{2,1,0:T(1,128)} %bitcast.5, s32[3,2048]{1,0:T(4,128)} %waves.1, f32[2048,128]{1,0:T(8,128)} %filt_hbm.1, f32[128,128]{1,0:T(8,128)} %wv.1, f32[128,128]{1,0:T(8,128)} %wc.1, f32[8,128]{1,0:T(8,128)} %mix.1, ...), custom_call_target="tpu_custom_call" | custom-call | tf_op jit(solution)/shard_map/layer/pallas_call | solution.py:562
  74.3 1.7 %copy.13 = f32[2,2,1,128,128]{4,3,2,1,0:T(8,128)} copy(f32[2,2,1,128,128]{4,3,2,1,0:T(8,128)} %layer.1) | data formatting | bytes 524288
